TPU v7x, 32 devices: a whole 2x2x4 slice. The times are simulated.
32 devices in a mesh: expert: 8 (over z, core), hidden: 4 (over y, x).
Axes of the slice: x: 2, y: 2, z: 4, core: 2. Of those that a mesh axis runs over, the one named last changes fastest.
Arguments:
- inputs: bfloat16 [32768, 768], P(('expert', 'hidden')), may hold values from -6 to 6
- out_grad: bfloat16 [32768, 768], P(('expert', 'hidden')), may hold values from -6 to 6
- seq_lengths: int32 [32], P(('expert', 'hidden')), may hold values from 1 to 1024, 16384 in all
- routes: int32 [32768, 2], P(('expert', 'hidden')), may hold values from 0 to 15, all different within a row
- norm_master: float32 [4, 768], P(None, ('expert', 'hidden')), may hold values from 0.25 to 1.75
- norm_momentum: float32 [4, 768], P(None, ('expert', 'hidden')), may hold values from -768 to 768
- norm_average: float32 [4, 768], P(None, ('expert', 'hidden')), may hold values from 0.25 to 1.75
- qkv_master: float32 [768, 2304], P(('expert', 'hidden')), may hold values from -0.21875 to 0.21875
- qkv_momentum: float32 [768, 2304], P(('expert', 'hidden')), may hold values from -512 to 512
- qkv_average: float32 [768, 2304], P(('expert', 'hidden')), may hold values from -0.21875 to 0.21875
- proj_master: float32 [768, 768], P(None, ('expert', 'hidden')), may hold values from -1.75 to 1.75
- proj_momentum: float32 [768, 768], P(None, ('expert', 'hidden')), may hold values from -112 to 112
- proj_average: float32 [768, 768], P(None, ('expert', 'hidden')), may hold values from -1.75 to 1.75
- router_master: float32 [768, 16], P(('expert', 'hidden')), may hold values from -0.21875 to 0.21875
- router_momentum: float32 [768, 16], P(('expert', 'hidden')), may hold values from -1536 to 1536
- router_average: float32 [768, 16], P(('expert', 'hidden')), may hold values from -0.21875 to 0.21875
- frozen_in: bfloat16 [8, 768, 3072], P('expert', None, 'hidden'), may hold values from -0.21875 to 0.21875
- frozen_out: bfloat16 [8, 3072, 768], P('expert', 'hidden'), may hold values from -0.109375 to 0.109375
- expert_in_master: float32 [8, 768, 3072], P('expert', None, 'hidden'), may hold values from -0.21875 to 0.21875
- expert_in_momentum: float32 [8, 768, 3072], P('expert', None, 'hidden'), may hold values from -28 to 28
- expert_in_average: float32 [8, 768, 3072], P('expert', None, 'hidden'), may hold values from -0.21875 to 0.21875
- expert_out_master: float32 [8, 3072, 768], P('expert', 'hidden'), may hold values from -0.109375 to 0.109375
- expert_out_momentum: float32 [8, 3072, 768], P('expert', 'hidden'), may hold values from -56 to 56
- expert_out_average: float32 [8, 3072, 768], P('expert', 'hidden'), may hold values from -0.109375 to 0.109375
Outputs:
- outputs: bfloat16 [32768, 768], P(('expert', 'hidden'))
- input_grad: float32 [32768, 768], P(('expert', 'hidden'))
- norm_grad: float32 [4, 768], P(None, ('expert', 'hidden'))
- norm_moment: float32 [4, 768], P(None, ('expert', 'hidden'))
- norm_weight: float32 [4, 768], P(None, ('expert', 'hidden'))
- norm_ema: float32 [4, 768], P(None, ('expert', 'hidden'))
- qkv_grad: float32 [768, 2304], P(('expert', 'hidden'))
- qkv_moment: float32 [768, 2304], P(('expert', 'hidden'))
- qkv_weight: float32 [768, 2304], P(('expert', 'hidden'))
- qkv_ema: float32 [768, 2304], P(('expert', 'hidden'))
- proj_grad: float32 [768, 768], P(None, ('expert', 'hidden'))
- proj_moment: float32 [768, 768], P(None, ('expert', 'hidden'))
- proj_weight: float32 [768, 768], P(None, ('expert', 'hidden'))
- proj_ema: float32 [768, 768], P(None, ('expert', 'hidden'))
- router_grad: float32 [768, 16], P(('expert', 'hidden'))
- router_moment: float32 [768, 16], P(('expert', 'hidden'))
- router_weight: float32 [768, 16], P(('expert', 'hidden'))
- router_ema: float32 [768, 16], P(('expert', 'hidden'))
- expert_in_grad: float32 [8, 768, 3072], P('expert', None, 'hidden')
- expert_in_moment: float32 [8, 768, 3072], P('expert', None, 'hidden')
- expert_in_weight: float32 [8, 768, 3072], P('expert', None, 'hidden')
- expert_in_ema: float32 [8, 768, 3072], P('expert', None, 'hidden')
- expert_out_grad: float32 [8, 3072, 768], P('expert', 'hidden')
- expert_out_moment: float32 [8, 3072, 768], P('expert', 'hidden')
- expert_out_weight: float32 [8, 3072, 768], P('expert', 'hidden')
- expert_out_ema: float32 [8, 3072, 768], P('expert', 'hidden')
Inputs may be any that keep to these rules, and one draw needn't show every extreme that they name: `seq_lengths`: the longest sequence has exactly 1024 tokens and the lengths sum to 16384. `routes`: the two experts of a token differ, and every expert is named by some token.
All inputs are finite; a program needn't handle non-finite values. No bound on the sum of `seq_lengths` on one device may be relied on, other than what follows from the above.
Results may differ from a plain program's by a relative error of at most 0.015.
The roundings to bfloat16 on the way count: a program that leaves them out, or rounds other values in their place, can miss the bound.
Values may be sent and summed in bfloat16 or wider, within the bound.
No kernel may reach another device: no remote copies, remote signals or barrier semaphores. Data moves between devices by JAX's collectives and lax.ppermute only.
A program may use at most 320 MiB of HBM per device.

v0:
```python
import math

import jax
import jax.numpy as jnp
from jax import lax
from jax.sharding import PartitionSpec as P

HEADS = 12
HEAD_DIM = 64
FF = 3072


EPSILON = 1e-05
MOMENT = 0.9
KEEP_MEAN = 0.75
MASKED = -1e30


def layer_norm(values, gain_row, shift_row):
    row_mean = jnp.mean(values, axis=-1, keepdims=True)
    centered = values - row_mean
    inverse = lax.rsqrt(jnp.mean(centered * centered, axis=-1, keepdims=True) + EPSILON)
    normed = centered * inverse
    return (normed * gain_row + shift_row, normed, inverse)


def norm_back(grad_rows, normed, inverse, gain_row):
    scaled = grad_rows * gain_row
    first_mean = jnp.mean(scaled, axis=-1, keepdims=True)
    second_mean = jnp.mean(scaled * normed, axis=-1, keepdims=True)
    grad_in = inverse * (scaled - first_mean - normed * second_mean)
    return (grad_in, jnp.sum(grad_rows * normed, axis=0), jnp.sum(grad_rows, axis=0))


def gelu_grad(pre_act, grad_act):
    pullback = jax.vjp(jax.nn.gelu, pre_act)[1]
    return pullback(grad_act)[0]


def block_mask(row_start, block_rows, key_count, length):
    query_pos = row_start + jnp.arange(block_rows, dtype=jnp.int32)
    key_pos = jnp.arange(key_count, dtype=jnp.int32)
    return (key_pos[None, :] <= query_pos[:, None]) & (key_pos[None, :] < length)


def attend_forward(queries, key_rows, value_rows, length, block_rows, score_scale):
    seq_len = queries.shape[0]

    def one_block(block_index):
        row_start = block_index * block_rows
        query_part = lax.dynamic_slice_in_dim(queries, row_start, block_rows, 0)
        scores = (
            jnp.einsum("qhd,khd->hqk", query_part, key_rows, preferred_element_type=jnp.float32)
            * score_scale
        )
        scores = jnp.where(block_mask(row_start, block_rows, seq_len, length)[None], scores, MASKED)
        row_peak = jnp.max(scores, axis=-1, keepdims=True)
        expo_terms = jnp.exp(scores - row_peak)
        row_total = jnp.sum(expo_terms, axis=-1, keepdims=True)
        probabilities = (expo_terms / row_total).astype(jnp.bfloat16)
        mixed_rows = jnp.einsum(
            "hqk,khd->qhd", probabilities, value_rows, preferred_element_type=jnp.float32
        )
        return (mixed_rows.astype(jnp.bfloat16), (row_peak + jnp.log(row_total))[..., 0])

    return lax.map(one_block, jnp.arange(seq_len // block_rows, dtype=jnp.int32))


def attend_backward(
    queries, key_rows, value_rows, grad_mixed, log_totals, length, block_rows, score_scale
):
    seq_len = queries.shape[0]

    def one_block(carried, block_index):
        grad_keys, grad_values = carried
        row_start = block_index * block_rows
        query_part = lax.dynamic_slice_in_dim(queries, row_start, block_rows, 0)
        grad_part = lax.dynamic_slice_in_dim(grad_mixed, row_start, block_rows, 0)
        scores = (
            jnp.einsum("qhd,khd->hqk", query_part, key_rows, preferred_element_type=jnp.float32)
            * score_scale
        )
        allowed = block_mask(row_start, block_rows, seq_len, length)[None]
        probabilities = jnp.where(
            allowed, jnp.exp(scores - log_totals[block_index][..., None]), 0.0
        )
        grad_probs = jnp.einsum(
            "qhd,khd->hqk", grad_part, value_rows, preferred_element_type=jnp.float32
        )
        row_dot = jnp.sum(probabilities * grad_probs, axis=-1, keepdims=True)
        grad_scores = (probabilities * (grad_probs - row_dot)).astype(jnp.bfloat16)
        grad_query = (
            jnp.einsum("hqk,khd->qhd", grad_scores, key_rows, preferred_element_type=jnp.float32)
            * score_scale
        )
        grad_keys = (
            grad_keys
            + jnp.einsum(
                "hqk,qhd->khd", grad_scores, query_part, preferred_element_type=jnp.float32
            )
            * score_scale
        )
        grad_values = grad_values + jnp.einsum(
            "hqk,qhd->khd",
            probabilities.astype(jnp.bfloat16),
            grad_part,
            preferred_element_type=jnp.float32,
        )
        return ((grad_keys, grad_values), grad_query)

    zero_acc = jnp.zeros(key_rows.shape, jnp.float32)
    sums, grad_queries = lax.scan(
        one_block, (zero_acc, zero_acc), jnp.arange(seq_len // block_rows, dtype=jnp.int32)
    )
    return (grad_queries.reshape(queries.shape), sums[0], sums[1])


def nesterov(master, momentum, average, grad_full, rate):
    moment_new = MOMENT * momentum + grad_full
    weight_new = master - rate * (grad_full + MOMENT * moment_new)
    return (grad_full, moment_new, weight_new, KEEP_MEAN * average + (1.0 - KEEP_MEAN) * weight_new)


def per_device(
    inputs,
    out_grad,
    seq_lengths,
    routes,
    norm_master,
    norm_momentum,
    norm_average,
    qkv_master,
    qkv_momentum,
    qkv_average,
    proj_master,
    proj_momentum,
    proj_average,
    router_master,
    router_momentum,
    router_average,
    frozen_in,
    frozen_out,
    expert_in_master,
    expert_in_momentum,
    expert_in_average,
    expert_out_master,
    expert_out_momentum,
    expert_out_average,
):
    tok_dev, model_width = inputs.shape
    seq_dev = seq_lengths.shape[0]
    seq_len = tok_dev // seq_dev
    n_expert = lax.axis_size("expert")
    n_hidden = lax.axis_size("hidden")
    experts = 2 * n_expert
    capacity = tok_dev * 2 // experts // 2
    slot_count = experts * capacity
    tokens_all = tok_dev * n_expert * n_hidden
    block_rows = min(512, seq_len)
    score_scale = HEAD_DIM ** (-0.5)
    shared = (
        lax.all_gather(norm_master.astype(jnp.bfloat16), ("expert", "hidden"), axis=1, tiled=True),
        lax.all_gather(qkv_master.astype(jnp.bfloat16), ("expert", "hidden"), axis=0, tiled=True),
        lax.all_gather(proj_master.astype(jnp.bfloat16), ("expert", "hidden"), axis=1, tiled=True),
        lax.all_gather(
            router_master.astype(jnp.bfloat16), ("expert", "hidden"), axis=0, tiled=True
        ),
    )
    norm_full = shared[0].astype(jnp.float32)
    qkv_full = shared[1]
    proj_full = shared[2]
    router_full = shared[3]
    row_ids = jnp.arange(tok_dev, dtype=jnp.int32)
    row_length = jnp.repeat(seq_lengths, seq_len, total_repeat_length=tok_dev)
    live_rows = row_ids % seq_len < row_length
    live_float = live_rows.astype(jnp.float32)[:, None]
    resid_in = inputs.astype(jnp.float32)
    normed_one, base_one, inverse_one = layer_norm(resid_in, norm_full[0], norm_full[1])
    attn_in = normed_one.astype(jnp.bfloat16)
    qkv_rows = jnp.dot(attn_in, qkv_full, preferred_element_type=jnp.float32).astype(jnp.bfloat16)
    shaped = qkv_rows.reshape(seq_dev, seq_len, 3, HEADS, HEAD_DIM)
    queries = shaped[:, :, 0]
    key_rows = shaped[:, :, 1]
    value_rows = shaped[:, :, 2]

    def forward_seq(items):
        return attend_forward(items[0], items[1], items[2], items[3], block_rows, score_scale)

    mixed_blocks, log_totals = lax.map(forward_seq, (queries, key_rows, value_rows, seq_lengths))
    attn_out = mixed_blocks.reshape(tok_dev, model_width)
    branch = jnp.dot(attn_out, proj_full, preferred_element_type=jnp.float32)
    resid_mid = resid_in + branch
    normed_two, base_two, inverse_two = layer_norm(resid_mid, norm_full[2], norm_full[3])
    moe_in = normed_two.astype(jnp.bfloat16)
    logits = jnp.dot(moe_in, router_full, preferred_element_type=jnp.float32)
    gates = jax.nn.softmax(jnp.take_along_axis(logits, routes, axis=1), axis=-1)
    flat_route = routes.reshape(-1)
    pair_live = jnp.repeat(live_rows, 2)
    expert_ids = jnp.arange(experts, dtype=jnp.int32)
    onehot = ((flat_route[:, None] == expert_ids[None, :]) & pair_live[:, None]).astype(jnp.int32)
    pair_rank = jnp.sum((jnp.cumsum(onehot, axis=0) - onehot) * onehot, axis=1)
    kept_pair = pair_live & (pair_rank < capacity)
    kept_float = kept_pair.astype(jnp.float32)
    slot_index = (
        flat_route // 2 * capacity + jnp.minimum(pair_rank, capacity - 1)
    ) * 2 + flat_route % 2
    target = jnp.where(kept_pair, slot_index, slot_count)
    pair_ids = jnp.arange(2 * tok_dev, dtype=jnp.int32)
    slot_pair = (
        jnp.full((slot_count + 1,), 2 * tok_dev, jnp.int32).at[target].set(pair_ids)[:slot_count]
    )
    padded_in = jnp.concatenate([moe_in, jnp.zeros((1, model_width), jnp.bfloat16)], axis=0)
    send_rows = padded_in[slot_pair // 2].reshape(n_expert, capacity, 2, model_width)
    slot_rows = lax.all_to_all(
        send_rows, "expert", split_axis=0, concat_axis=0, tiled=True
    ).reshape(n_expert * capacity, 2, model_width)
    weight_in = jnp.concatenate([frozen_in, expert_in_master.astype(jnp.bfloat16)], axis=0)
    weight_out = jnp.concatenate([frozen_out, expert_out_master.astype(jnp.bfloat16)], axis=0)
    group_rows = lax.all_gather(slot_rows, "hidden", axis=0, tiled=True)
    pre_act = jnp.einsum("rld,ldf->rlf", group_rows, weight_in, preferred_element_type=jnp.float32)
    activation = jax.nn.gelu(pre_act).astype(jnp.bfloat16)
    piece_rows = activation
    expert_sum = lax.psum_scatter(
        jnp.einsum("rlf,lfd->rld", piece_rows, weight_out, preferred_element_type=jnp.float32),
        "hidden",
        scatter_dimension=0,
        tiled=True,
    )
    back_rows = lax.all_to_all(
        expert_sum.astype(jnp.bfloat16).reshape(n_expert, capacity, 2, model_width),
        "expert",
        split_axis=0,
        concat_axis=0,
        tiled=True,
    ).reshape(slot_count, model_width)
    pair_out = back_rows[slot_index].astype(jnp.float32)
    pair_weight = gates.reshape(-1) * kept_float
    moe_out = jnp.sum((pair_out * pair_weight[:, None]).reshape(tok_dev, 2, model_width), axis=1)
    outputs = (live_float * (resid_mid + moe_out)).astype(jnp.bfloat16)
    grad_out = out_grad.astype(jnp.float32) * live_float
    grad_pairs = jnp.repeat(grad_out, 2, axis=0)
    grad_gate = kept_float * jnp.sum(grad_pairs * pair_out, axis=1)
    pair_grad = (grad_pairs * pair_weight[:, None]).astype(jnp.bfloat16)
    padded_grad = jnp.concatenate([pair_grad, jnp.zeros((1, model_width), jnp.bfloat16)], axis=0)
    send_grad = padded_grad[slot_pair].reshape(n_expert, capacity, 2, model_width)
    grad_slots = lax.all_to_all(
        send_grad, "expert", split_axis=0, concat_axis=0, tiled=True
    ).reshape(n_expert * capacity, 2, model_width)
    grad_group = lax.all_gather(grad_slots, "hidden", axis=0, tiled=True)
    grad_act = jnp.einsum(
        "rld,lfd->rlf", grad_group, weight_out, preferred_element_type=jnp.float32
    )
    grad_pre = gelu_grad(pre_act, grad_act).astype(jnp.bfloat16)
    grad_w_out = jnp.einsum(
        "rf,rd->fd", activation[:, 1], grad_group[:, 1], preferred_element_type=jnp.float32
    )
    grad_w_in = jnp.einsum(
        "rd,rf->df", group_rows[:, 1], grad_pre[:, 1], preferred_element_type=jnp.float32
    )
    piece_rows = grad_pre
    grad_rows = lax.psum_scatter(
        jnp.einsum("rlf,ldf->rld", piece_rows, weight_in, preferred_element_type=jnp.float32),
        "hidden",
        scatter_dimension=0,
        tiled=True,
    )
    grad_back = lax.all_to_all(
        grad_rows.astype(jnp.bfloat16).reshape(n_expert, capacity, 2, model_width),
        "expert",
        split_axis=0,
        concat_axis=0,
        tiled=True,
    ).reshape(slot_count, model_width)
    grad_moe_in = jnp.sum(
        (grad_back[slot_index].astype(jnp.float32) * kept_float[:, None]).reshape(
            tok_dev, 2, model_width
        ),
        axis=1,
    )
    gate_grad = grad_gate.reshape(tok_dev, 2)
    grad_chosen = gates * (gate_grad - jnp.sum(gates * gate_grad, axis=1, keepdims=True))
    route_match = routes[:, :, None] == expert_ids[None, None, :]
    grad_logits = jnp.sum(jnp.where(route_match, grad_chosen[:, :, None], 0.0), axis=1).astype(
        jnp.bfloat16
    )
    router_part = jnp.einsum("td,te->de", moe_in, grad_logits, preferred_element_type=jnp.float32)
    grad_norm_two = (
        jnp.einsum("te,de->td", grad_logits, router_full, preferred_element_type=jnp.float32)
        + grad_moe_in
    )
    grad_low_two, gain_two_grad, shift_two_grad = norm_back(
        grad_norm_two, base_two, inverse_two, norm_full[2]
    )
    grad_mid = grad_out + grad_low_two
    grad_branch = grad_mid.astype(jnp.bfloat16)
    proj_part = jnp.einsum("td,te->de", attn_out, grad_branch, preferred_element_type=jnp.float32)
    grad_attn = jnp.einsum(
        "te,de->td", grad_branch, proj_full, preferred_element_type=jnp.float32
    ).astype(jnp.bfloat16)

    def backward_seq(items):
        return attend_backward(
            items[0], items[1], items[2], items[3], items[4], items[5], block_rows, score_scale
        )

    grad_q, grad_k, grad_v = lax.map(
        backward_seq,
        (
            queries,
            key_rows,
            value_rows,
            grad_attn.reshape(seq_dev, seq_len, HEADS, HEAD_DIM),
            log_totals,
            seq_lengths,
        ),
    )
    grad_qkv = (
        jnp.stack([grad_q, grad_k, grad_v], axis=2)
        .reshape(tok_dev, 3 * model_width)
        .astype(jnp.bfloat16)
    )
    qkv_part = jnp.einsum("td,te->de", attn_in, grad_qkv, preferred_element_type=jnp.float32)
    grad_norm_one = jnp.einsum("te,de->td", grad_qkv, qkv_full, preferred_element_type=jnp.float32)
    grad_low_one, gain_one_grad, shift_one_grad = norm_back(
        grad_norm_one, base_one, inverse_one, norm_full[0]
    )
    input_grad = grad_mid + grad_low_one
    norm_part = jnp.stack([gain_one_grad, shift_one_grad, gain_two_grad, shift_two_grad])
    norm_sum, qkv_sum, proj_sum, router_sum = (
        lax.psum_scatter(norm_part, ("expert", "hidden"), scatter_dimension=1, tiled=True),
        lax.psum_scatter(qkv_part, ("expert", "hidden"), scatter_dimension=0, tiled=True),
        lax.psum_scatter(proj_part, ("expert", "hidden"), scatter_dimension=1, tiled=True),
        lax.psum_scatter(router_part, ("expert", "hidden"), scatter_dimension=0, tiled=True),
    )
    norm_rate = 0.1 / math.sqrt(tokens_all)
    qkv_rate = 1.0 / math.sqrt(model_width * tokens_all)
    proj_rate = 40.0 / math.sqrt(model_width * tokens_all)
    router_rate = 0.08 * math.sqrt(experts / (model_width * tokens_all))
    in_rate = 5.0 * math.sqrt(experts / (model_width * tokens_all))
    out_rate = 2.5 * math.sqrt(experts / (FF * tokens_all))
    norm_set = nesterov(norm_master, norm_momentum, norm_average, norm_sum, norm_rate)
    qkv_set = nesterov(qkv_master, qkv_momentum, qkv_average, qkv_sum, qkv_rate)
    proj_set = nesterov(proj_master, proj_momentum, proj_average, proj_sum, proj_rate)
    router_set = nesterov(router_master, router_momentum, router_average, router_sum, router_rate)
    in_set = nesterov(
        expert_in_master, expert_in_momentum, expert_in_average, grad_w_in[None], in_rate
    )
    out_set = nesterov(
        expert_out_master, expert_out_momentum, expert_out_average, grad_w_out[None], out_rate
    )
    return (
        outputs,
        input_grad,
        norm_set[0],
        norm_set[1],
        norm_set[2],
        norm_set[3],
        qkv_set[0],
        qkv_set[1],
        qkv_set[2],
        qkv_set[3],
        proj_set[0],
        proj_set[1],
        proj_set[2],
        proj_set[3],
        router_set[0],
        router_set[1],
        router_set[2],
        router_set[3],
        in_set[0],
        in_set[1],
        in_set[2],
        in_set[3],
        out_set[0],
        out_set[1],
        out_set[2],
        out_set[3],
    )


def solution(mesh):
    return jax.shard_map(
        per_device,
        mesh=mesh,
        in_specs=(
            P(("expert", "hidden"), None),
            P(("expert", "hidden"), None),
            P(("expert", "hidden")),
            P(("expert", "hidden"), None),
            P(None, ("expert", "hidden")),
            P(None, ("expert", "hidden")),
            P(None, ("expert", "hidden")),
            P(("expert", "hidden"), None),
            P(("expert", "hidden"), None),
            P(("expert", "hidden"), None),
            P(None, ("expert", "hidden")),
            P(None, ("expert", "hidden")),
            P(None, ("expert", "hidden")),
            P(("expert", "hidden"), None),
            P(("expert", "hidden"), None),
            P(("expert", "hidden"), None),
            P("expert", None, "hidden"),
            P("expert", "hidden", None),
            P("expert", None, "hidden"),
            P("expert", None, "hidden"),
            P("expert", None, "hidden"),
            P("expert", "hidden", None),
            P("expert", "hidden", None),
            P("expert", "hidden", None),
        ),
        out_specs=(
            P(("expert", "hidden"), None),
            P(("expert", "hidden"), None),
            P(None, ("expert", "hidden")),
            P(None, ("expert", "hidden")),
            P(None, ("expert", "hidden")),
            P(None, ("expert", "hidden")),
            P(("expert", "hidden"), None),
            P(("expert", "hidden"), None),
            P(("expert", "hidden"), None),
            P(("expert", "hidden"), None),
            P(None, ("expert", "hidden")),
            P(None, ("expert", "hidden")),
            P(None, ("expert", "hidden")),
            P(None, ("expert", "hidden")),
            P(("expert", "hidden"), None),
            P(("expert", "hidden"), None),
            P(("expert", "hidden"), None),
            P(("expert", "hidden"), None),
            P("expert", None, "hidden"),
            P("expert", None, "hidden"),
            P("expert", None, "hidden"),
            P("expert", None, "hidden"),
            P("expert", "hidden", None),
            P("expert", "hidden", None),
            P("expert", "hidden", None),
            P("expert", "hidden", None),
        ),
        check_vma=False,
    )
```

profile of v0, /device:TPU:0, one launch (start us, length us, event | category | flops | bytes accessed | tf_op | source)
XLA Modules:
  0.0 1332.5 jit_solution(7554052428411498812)
XLA Ops:
  20.8 69.8 %all-gather = bf16[32,24,4]{1,2,0:T(4,128)(2,1)S(1)} all-gather(bf16[1,24,4]{1,2,0:T(4,128)(2,1)S(1)} %convert_bitcast_fusion.3), channel_id=1, replica_groups=mesh['expert'=8,'hidden'=4] {'expert','hidden'}, dimensions={0}, use_global_device_ids=true | all-gather | bytes 6336 | tf_op jit(solution)/shard_map/all_gather | solution.py:162
  120.1 74.1 %while.49 = (s32[]{:T(128)}, bf16[2,512,12,64]{1,3,2,0:T(8,128)(2,1)}, f32[2,12,512]{2,1,0:T(8,128)S(1)}, s32[2]{0:T(128)S(1)}, s32[]{:T(128)}, /*index=5*/bf16[...) while((s32[]{:T(128)}, ...), condition=%wide.region_5.6_spmd, body=%wide.region_2.5_spmd.sunk | while | flops 1687547392 | bytes 189495552 | solution.py:66
  122.4 10.7 fusion.153
  133.2 12.3 fusion.154
  159.4 10.7 fusion.153
  170.1 12.3 fusion.154
  214.7 40.3 %all_to_all.20 = bf16[8,64,2,768]{3,1,2,0:T(8,128)(2,1)S(1)} all-to-all(bf16[8,64,2,768]{3,1,2,0:T(8,128)(2,1)S(1)} %copy.178), channel_id=1, replica_groups=mesh['expert'=8,'hidden'=4] {'expert'}, dimensions={0} | all-to-all | bytes 3145728 | tf_op jit(solution)/shard_map/all_to_all | solution.py:214
  266.4 57.2 %all-gather.11.cloned.1.call-done = bf16[2048,2,768]{2,0,1:T(8,128)(2,1)} async-done(((bf16[512,2,768]{2,0,1:T(8,128)(2,1)}), bf16[2048,2,768]{2,0,1:T(8,128)(2,1)}) %all-gather.11.cloned.1.call-update) | async-done | bytes 6291472 | tf_op jit(solution)/shard_map/all_gather | solution.py:219
  323.6 12.7 fusion.41
  346.9 120.9 %reduce-scatter.7.cloned.1.call-done = f32[512,2,768]{0,2,1:T(8,128)} async-done(((f32[2048,2,768]{0,2,1:T(8,128)}), f32[512,2,768]{0,2,1:T(8,128)}) %reduce-scatter.7.cloned.1.call-update) | async-done | bytes 3145744 | tf_op jit(solution)/shard_map/reduce_scatter | solution.py:223
  479.3 88.4 %all-gather.1 = bf16[32,24,16]{1,2,0:T(8,128)(2,1)S(1)} all-gather(bf16[1,24,16]{1,2,0:T(8,128)(2,1)S(1)} %convert_bitcast_fusion.2), channel_id=1, replica_groups=mesh['expert'=8,'hidden'=4] {'expert','hidden'}, dimensions={0}, use_global_device_ids=true | all-gather | bytes 25344 | tf_op jit(solution)/shard_map/all_gather | solution.py:165
  585.5 16.8 %gather_fusion.4 = f32[2048]{0:T(1024)S(1)} fusion(f32[1024,16]{0,1:T(8,128)S(1)} %fusion.106, s32[2048]{0:T(1024)S(1)} %reshape.726), kind=kCustom, calls=%fused_computation.4 | custom fusion | bytes 32768 | tf_op jit(solution)/shard_map/jit(take_along_axis)/gather | solution.py:196
  634.7 40.3 %all_to_all.21 = bf16[8,64,2,768]{3,1,2,0:T(8,128)(2,1)S(1)} all-to-all(bf16[8,64,2,768]{3,1,2,0:T(8,128)(2,1)S(1)} %copy.191), channel_id=1, replica_groups=mesh['expert'=8,'hidden'=4] {'expert'}, dimensions={0} | all-to-all | bytes 3145728 | tf_op jit(solution)/shard_map/all_to_all | solution.py:246
  676.3 67.9 %all-gather.13.cloned.1.call-done = bf16[2048,2,768]{2,0,1:T(8,128)(2,1)} async-done(((bf16[512,2,768]{2,0,1:T(8,128)(2,1)}), bf16[2048,2,768]{2,0,1:T(8,128)(2,1)}) %all-gather.13.cloned.1.call-update) | async-done | bytes 6291472 | tf_op jit(solution)/shard_map/all_gather | solution.py:249
  744.2 17.0 %fusion.37 = bf16[2048,2,768]{0,2,1:T(8,128)(2,1)S(1)} fusion(f32[2,768,2048]{2,1,0:T(8,128)} %get-tuple-element.338, bf16[2048,2,768]{2,0,1:T(8,128)(2,1)} %all-gather.13.cloned.1.call-done, bf16[1,768,768]{1,2,0:T(8,128)(2,1)} %copy.168, bf16[1,768,768]{1,2,0:T(8,128)(2,1)} %copy.169), kind=kOutput, calls=%fused_computation.59 | convolution fusion | flops 4895932416 | bytes 27525120 | tf_op jit(solution)/shard_map/rld,lfd->rlf/dot_general | solution.py:250
  773.2 120.9 %reduce-scatter.9.cloned.1.call-done = f32[512,2,768]{0,2,1:T(8,128)} async-done(((f32[2048,2,768]{0,2,1:T(8,128)}), f32[512,2,768]{0,2,1:T(8,128)}) %reduce-scatter.9.cloned.1.call-update) | async-done | bytes 3145744 | tf_op jit(solution)/shard_map/reduce_scatter | solution.py:261
  911.8 11.2 multiply_reduce_fusion.3
  923.0 20.2 %all-to-all-done.3 = bf16[8,64,2,768]{3,1,2,0:T(8,128)(2,1)} async-done(((bf16[8,64,2,768]{3,1,2,0:T(8,128)(2,1)}), bf16[8,64,2,768]{3,1,2,0:T(8,128)(2,1)}, u32[]{:S(2)}, u32[]{:S(2)}) %all-to-all-start.3) | async-done | bytes 1572896 | tf_op jit(solution)/shard_map/all_to_all | solution.py:267
  964.2 31.2 %multiply_reduce_fusion.1 = f32[1024,768]{1,0:T(8,128)S(1)} fusion(f32[1024,2,768]{2,1,0:T(2,128)} %reshape.693, f32[1024,2]{1,0:T(8,128)S(1)} %copy-done.23), kind=kLoop, calls=%fused_computation.67 | loop fusion | flops 2359296 | bytes 9445376 | tf_op jit(solution)/shard_map/reduce_sum | solution.py:274
  1009.7 175.8 %while.50 = (s32[]{:T(128)}, f32[1024,12,64]{0,2,1:T(8,128)}, f32[1024,12,64]{0,2,1:T(8,128)}, bf16[2,512,12,64]{1,3,2,0:T(8,128)(2,1)}, s32[2]{0:T(128)S(1)}, /...) while((s32[]{:T(128)}, f32[1024,12,64]{0,2,1:T(8,128)}, ...), condition=%wide.region_25.26_spmd.clone, body=%wide.region_23.25_spmd.clone.sunk | while | flops 4126273024 | bytes 225630544 | solution.py:112
  1014.2 11.7 fusion.165
  1025.9 13.2 bitcast_add_fusion.5
  1039.1 18.2 %multiply_reduce_fusion.11 = (f32[12,512]{1,0:T(8,128)S(1)}, f32[12,512,1024]{2,1,0:T(8,128)}) fusion(f32[12,512,1024]{2,1,0:T(8,128)} %fusion.165, f32[12,512]{1,0:T(8,128)S(1)} %dynamic-slice_bitcast_fusion.2, pred[512,1024]{1,0:T(8,128)(4,1)S(1)} %fusion.166, bf16[1024,12,64]{0,2,1:T(8,128)(2,1)} %get-tuple-element.547, ...), kind=kOutput, calls=%fused_computation.26.clone.1 | convolution fusion | flops 836757504 | bytes 53264388 | tf_op jit(solution)/shard_map/while/body/eval_jaxpr/while/body/eval_jaxpr/qhd,khd->hqk/dot_general | solution.py:87
  1057.3 21.9 %multiply_convert_fusion.4 = bf16[12,512,1024]{2,1,0:T(8,128)(2,1)} fusion(f32[12,512,1024]{2,1,0:T(8,128)} %get-tuple-element.467, f32[12,512,1024]{2,1,0:T(8,128)} %fusion.165, f32[12,512]{1,0:T(8,128)S(1)} %get-tuple-element.468, f32[12,512]{1,0:T(8,128)S(1)} %dynamic-slice_bitcast_fusion.2, pred[512,1024]{1,0:T(8,128)(4,1)S(1)} %fusion.166), kind=kLoop, calls=%fused_computation.25.clone.1 | loop fusion | flops 37748736 | bytes 63488000 | tf_op jit(solution)/shard_map/while/body/eval_jaxpr/while/body/eval_jaxpr/convert_element_type | solution.py:91
  1079.2 9.6 bitcast_dynamic-update-slice_fusion.5
  1101.7 11.4 fusion.165
  1113.1 13.9 %bitcast_add_fusion.5 = f32[1024,12,64]{0,2,1:T(8,128)} fusion(f32[1024,12,64]{0,2,1:T(8,128)} %get-tuple-element.523, f32[12,512,1024]{2,1,0:T(8,128)} %fusion.165, f32[12,512]{1,0:T(8,128)S(1)} %dynamic-slice_bitcast_fusion.2, pred[512,1024]{1,0:T(8,128)(4,1)S(1)} %fusion.166, pred[]{:T(512)S(6)} %compare.38, ...), kind=kOutput, calls=%fused_computation.31.clone.1 | convolution fusion | flops 832045056 | bytes 32800772 | tf_op jit(solution)/shard_map/while/body/eval_jaxpr/while/body/eval_jaxpr/hqk,qhd->khd/dot_general | solution.py:103
  1127.0 18.1 %multiply_reduce_fusion.11 = (f32[12,512]{1,0:T(8,128)S(1)}, f32[12,512,1024]{2,1,0:T(8,128)}) fusion(f32[12,512,1024]{2,1,0:T(8,128)} %fusion.165, f32[12,512]{1,0:T(8,128)S(1)} %dynamic-slice_bitcast_fusion.2, pred[512,1024]{1,0:T(8,128)(4,1)S(1)} %fusion.166, bf16[1024,12,64]{0,2,1:T(8,128)(2,1)} %get-tuple-element.547, ...), kind=kOutput, calls=%fused_computation.26.clone.1 | convolution fusion | flops 836757504 | bytes 53264388 | tf_op jit(solution)/shard_map/while/body/eval_jaxpr/while/body/eval_jaxpr/qhd,khd->hqk/dot_general | solution.py:87
  1145.2 21.1 %multiply_convert_fusion.4 = bf16[12,512,1024]{2,1,0:T(8,128)(2,1)} fusion(f32[12,512,1024]{2,1,0:T(8,128)} %get-tuple-element.467, f32[12,512,1024]{2,1,0:T(8,128)} %fusion.165, f32[12,512]{1,0:T(8,128)S(1)} %get-tuple-element.468, f32[12,512]{1,0:T(8,128)S(1)} %dynamic-slice_bitcast_fusion.2, pred[512,1024]{1,0:T(8,128)(4,1)S(1)} %fusion.166), kind=kLoop, calls=%fused_computation.25.clone.1 | loop fusion | flops 37748736 | bytes 63488000 | tf_op jit(solution)/shard_map/while/body/eval_jaxpr/while/body/eval_jaxpr/convert_element_type | solution.py:91
  1207.4 12.8 multiply_add_fusion.1
  1236.8 38.8 %all-reduce.4 = (f32[4,768]{1,0:T(4,128)S(1)}, f32[768,16]{0,1:T(8,128)S(1)}) all-reduce(f32[4,768]{1,0:T(4,128)S(1)} %pad_maximum_fusion.7, f32[768,16]{0,1:T(8,128)S(1)} %fusion.107), channel_id=4, replica_groups=mesh['expert'=8,'hidden'=4] {'expert','hidden'}, use_global_device_ids=true, to_apply=%region_32.33.clone | all-reduce | flops 15360 | bytes 122880
  1283.4 39.9 %reduce-scatter.11.cloned.1.call-done = f32[24,2304]{1,0:T(8,128)} async-done(((f32[768,2304]{1,0:T(8,128)}), f32[24,2304]{1,0:T(8,128)}) %reduce-scatter.11.cloned.1.call-update) | async-done | bytes 221200 | tf_op jit(solution)/shard_map/reduce_scatter | solution.py:331
  (385 shorter events, 317.2 us)
Async XLA Ops:
  7.2 93.9 %all-gather.7.cloned.1.call-start = ((), (), s32[]{:S(2)}) async-start(), calls=%async_computation.8 | async-start | bytes 3649536 | tf_op jit(solution)/shard_map/all_gather | solution.py:163
  9.0 191.0 %all-gather.9.cloned.1.call-start = ((), (), s32[]{:S(2)}) async-start(), calls=%async_computation.9 | async-start | bytes 1216512 | tf_op jit(solution)/shard_map/all_gather | solution.py:164
  10.6 313.0 %all-gather.11.cloned.1.call-start = ((), (), s32[]{:S(2)}) async-start(), calls=%async_computation.10 | async-start | bytes 7864320 | tf_op jit(solution)/shard_map/all_gather | solution.py:219
  19.8 89.2 %copy-start.66 = (pred[2048]{0:T(1024)(128)(4,1)}, pred[2048]{0:T(1024)(128)(4,1)S(1)}, u32[]{:S(2)}) copy-start(pred[2048]{0:T(1024)(128)(4,1)S(1)} %broadcast_compare_fusion) | copy-start | bytes 6148
  20.2 88.9 %copy-start.56 = (f32[1024]{0:T(1024)}, f32[1024]{0:T(1024)S(1)}, u32[]{:S(2)}) copy-start(f32[1024]{0:T(1024)S(1)} %broadcast_multiply_fusion.5) | copy-start | bytes 12292
  20.8 88.2 %copy-start.70 = (f32[1024]{0:T(1024)}, f32[1024]{0:T(1024)S(1)}, u32[]{:S(2)}) copy-start(f32[1024]{0:T(1024)S(1)} %add_rsqrt_fusion.1) | copy-start | bytes 12292
  122.4 23.1 %copy-start.6 = (bf16[1024,12,64]{0,2,1:T(8,128)(2,1)S(1)}, bf16[1024,12,64]{0,2,1:T(8,128)(2,1)}, u32[]{:S(2)}) copy-start(bf16[1024,12,64]{0,2,1:T(8,128)(2,1)} %get-tuple-element.500) | copy-start | bytes 4718596 | tf_op jit(solution)/shard_map/while/body/eval_jaxpr/while
  205.6 379.4 %copy-start.10 = (bf16[1024,768]{1,0:T(8,128)(2,1)}, bf16[1024,768]{1,0:T(8,128)(2,1)S(1)}, u32[]{:S(2)}) copy-start(bf16[1024,768]{1,0:T(8,128)(2,1)S(1)} %add_convert_fusion) | copy-start | bytes 4718596
  256.3 211.5 %reduce-scatter.7.cloned.1.call-start = ((), (), s32[]{:S(2)}) async-start(), calls=%async_computation.11 | async-start | bytes 15728640 | tf_op jit(solution)/shard_map/reduce_scatter | solution.py:223
  263.2 73.1 %copy-start.27 = (bf16[1,768,768]{1,2,0:T(8,128)(2,1)}, bf16[1,768,768]{1,2,0:T(8,128)(2,1)S(1)}, u32[]{:S(2)}) copy-start(bf16[1,768,768]{1,2,0:T(8,128)(2,1)S(1)} %copy.170) | copy-start | bytes 3538948
  472.8 95.1 %copy-start.42 = (s32[1024,2]{0,1:T(2,128)S(1)}, s32[1024,2]{0,1:T(2,128)}, u32[]{:S(2)}) copy-start(s32[1024,2]{0,1:T(2,128)} %param.35) | copy-start | bytes 24580
  474.0 129.0 %all-to-all-start.1 = ((bf16[8,64,2,768]{3,1,2,0:T(8,128)(2,1)}), bf16[8,64,2,768]{3,1,2,0:T(8,128)(2,1)}, u32[]{:S(2)}, u32[]{:S(2)}) async-start(bf16[8,64,2,768]{3,1,2,0:T(8,128)(2,1)} %copy.182), calls=%async_computation.2 | async-start | bytes 3145728 | tf_op jit(solution)/shard_map/all_to_all | solution.py:229
  478.7 265.5 %all-gather.13.cloned.1.call-start = ((), (), s32[]{:S(2)}) async-start(), calls=%async_computation.12 | async-start | bytes 7864320 | tf_op jit(solution)/shard_map/all_gather | solution.py:249
  676.3 217.8 %reduce-scatter.9.cloned.1.call-start = ((), (), s32[]{:S(2)}) async-start(), calls=%async_computation.13 | async-start | bytes 15728640 | tf_op jit(solution)/shard_map/reduce_scatter | solution.py:261
  900.6 42.5 %all-to-all-start.3 = ((bf16[8,64,2,768]{3,1,2,0:T(8,128)(2,1)}), bf16[8,64,2,768]{3,1,2,0:T(8,128)(2,1)}, u32[]{:S(2)}, u32[]{:S(2)}) async-start(bf16[8,64,2,768]{3,1,2,0:T(8,128)(2,1)} %copy.197), calls=%async_computation.5 | async-start | bytes 3145728 | tf_op jit(solution)/shard_map/all_to_all | solution.py:267
  905.2 376.5 %reduce-scatter.13.cloned.1.call-start = ((), (), s32[]{:S(2)}) async-start(), calls=%async_computation.15 | async-start | bytes 2433024 | tf_op jit(solution)/shard_map/reduce_scatter | solution.py:332
  911.7 83.6 %copy-start.35 = (bf16[1024,16]{0,1:T(8,128)(2,1)}, bf16[1024,16]{0,1:T(8,128)(2,1)S(1)}, u32[]{:S(2)}) copy-start(bf16[1024,16]{0,1:T(8,128)(2,1)S(1)} %select_reduce_fusion) | copy-start | bytes 98308
  964.1 31.2 %copy-start.8 = (f32[1024,768]{1,0:T(8,128)S(1)}, f32[1024,768]{1,0:T(8,128)}, u32[]{:S(2)}) copy-start(f32[1024,768]{1,0:T(8,128)} %copy-done.7) | copy-start | bytes 9437188
  964.2 31.2 %copy-start.41 = (bf16[768,16]{0,1:T(8,128)(2,1)S(1)}, bf16[768,16]{0,1:T(8,128)(2,1)}, u32[]{:S(2)}) copy-start(bf16[768,16]{0,1:T(8,128)(2,1)} %copy-done.40) | copy-start | bytes 73732
  964.2 31.3 %copy-start.47 = (f32[1024]{0:T(1024)S(1)}, f32[1024]{0:T(1024)}, u32[]{:S(2)}) copy-start(f32[1024]{0:T(1024)} %copy-done.46) | copy-start | bytes 12292
  964.2 31.3 %copy-start.53 = (f32[768]{0:T(1024)S(1)}, f32[768]{0:T(1024)}, u32[]{:S(2)}) copy-start(f32[768]{0:T(1024)} %get-tuple-element.252) | copy-start | bytes 9220
  964.2 31.2 %copy-start.55 = (f32[1024]{0:T(1024)S(1)}, f32[1024]{0:T(1024)}, u32[]{:S(2)}) copy-start(f32[1024]{0:T(1024)} %copy-done.54) | copy-start | bytes 12292
  1005.0 318.3 %reduce-scatter.11.cloned.1.call-start = ((), (), s32[]{:S(2)}) async-start(), calls=%async_computation.14 | async-start | bytes 7299072 | tf_op jit(solution)/shard_map/reduce_scatter | solution.py:331
  1228.2 47.4 %copy-start.80 = (f32[4,24]{1,0:T(4,128)S(1)}, f32[4,24]{1,0:T(4,128)}, u32[]{:S(2)}) copy-start(f32[4,24]{1,0:T(4,128)} %param.36) | copy-start | bytes 1156
  1228.2 47.4 %copy-start.85 = (f32[4,24]{1,0:T(4,128)S(1)}, f32[4,24]{1,0:T(4,128)}, u32[]{:S(2)}) copy-start(f32[4,24]{1,0:T(4,128)} %param.38) | copy-start | bytes 1156
  1228.3 47.4 %copy-start.86 = (f32[4,24]{1,0:T(4,128)S(1)}, f32[4,24]{1,0:T(4,128)}, u32[]{:S(2)}) copy-start(f32[4,24]{1,0:T(4,128)} %param.37) | copy-start | bytes 1156
  1228.3 48.0 %copy-start.63 = (f32[24,16]{0,1:T(8,128)S(1)}, f32[24,16]{0,1:T(8,128)}, u32[]{:S(2)}) copy-start(f32[24,16]{0,1:T(8,128)} %param.45) | copy-start | bytes 4612
  1228.3 48.0 %copy-start.81 = (f32[24,16]{0,1:T(8,128)S(1)}, f32[24,16]{0,1:T(8,128)}, u32[]{:S(2)}) copy-start(f32[24,16]{0,1:T(8,128)} %param.47) | copy-start | bytes 4612
  1228.3 48.0 %copy-start.82 = (f32[24,16]{0,1:T(8,128)S(1)}, f32[24,16]{0,1:T(8,128)}, u32[]{:S(2)}) copy-start(f32[24,16]{0,1:T(8,128)} %param.46) | copy-start | bytes 4612
  1277.0 46.3 %copy-start.32 = (f32[24,2304]{1,0:T(8,128)S(1)}, f32[24,2304]{1,0:T(8,128)}, u32[]{:S(2)}) copy-start(f32[24,2304]{1,0:T(8,128)} %param.39) | copy-start | bytes 663556
  1277.0 46.3 %copy-start.38 = (f32[24,2304]{1,0:T(8,128)S(1)}, f32[24,2304]{1,0:T(8,128)}, u32[]{:S(2)}) copy-start(f32[24,2304]{1,0:T(8,128)} %param.41) | copy-start | bytes 663556
  1277.0 46.3 %copy-start.39 = (f32[24,2304]{1,0:T(8,128)S(1)}, f32[24,2304]{1,0:T(8,128)}, u32[]{:S(2)}) copy-start(f32[24,2304]{1,0:T(8,128)} %param.40) | copy-start | bytes 663556
  (75 other events, 544.6 us)
Sparse Core Ops, SparseCore 0:
  11.5 63.0 all-gather.6
  78.1 52.7 all-gather.8
  256.4 67.1 all-gather.10
  347.0 120.7 reduce-scatter.6
  676.4 67.7 all-gather.12
  773.4 120.7 reduce-scatter.8
  1005.1 96.9 reduce-scatter.12
  1205.8 117.5 reduce-scatter.10
where the time goes:
time: 1340 us; the launch traced here: 1330 us
  waiting for transfers between devices  427 us (32%)
  blocking collectives  277 us (21%)
  matrix products  267 us (20%)
  local copies, waits for them, and re-layouts  171 us (13%)
  other arithmetic  157 us (12%)
  between operations  16.6 us (1%)
    reduce_scatter x1, waiting for transfers between devices, per_device(): lax.psum_scatter(jnp.einsum('rlf,lfd->rld', piece_rows, weight_out, prefe...  121 us
    reduce_scatter x1, waiting for transfers between devices, per_device(): lax.psum_scatter(jnp.einsum('rlf,ldf->rld', piece_rows, weight_in, prefer...  121 us
    all_gather x1, blocking collectives, per_device(): lax.all_gather(router_master.astype(jnp.bfloat16), ('expert', 'hidden'),...  88.4 us
    all_gather x1, blocking collectives, per_device(): lax.all_gather(norm_master.astype(jnp.bfloat16), ('expert', 'hidden'), ax...  69.8 us
    all_gather x1, waiting for transfers between devices, per_device(): grad_group = lax.all_gather(grad_slots, 'hidden', axis=0, tiled=True)  67.9 us
    all_gather x1, waiting for transfers between devices, per_device(): group_rows = lax.all_gather(slot_rows, 'hidden', axis=0, tiled=True)  57.2 us
    dot_general x4, matrix products, one_block(): jnp.einsum('qhd,khd->hqk', query_part, key_rows, preferred_element_type=j...  44.6 us
    convert_element_type x2, other arithmetic, one_block(): grad_scores = (probabilities * (grad_probs - row_dot)).astype(jnp.bfloat16)  43.1 us
  transfers between devices with their start and end apart: 10, of which 6 were waited for; matrix products, arithmetic and copies ran while one was open for 30% of the time, Pallas kernels for 0%

commit v1 on v0

v1 whole, which is shorter than its diff:
```python
import functools
import math

import jax
import jax.numpy as jnp
from jax import lax
from jax.experimental import pallas as pl
from jax.experimental.pallas import tpu as pltpu
from jax.sharding import PartitionSpec as P

HEADS = 12
HEAD_DIM = 64
FF = 3072


EPSILON = 1e-05
MOMENT = 0.9
KEEP_MEAN = 0.75
MASKED = -1e30

BF16 = jnp.bfloat16
F32 = jnp.float32
NN = (((1,), (0,)), ((), ()))
NT = (((1,), (1,)), ((), ()))
TN = (((0,), (0,)), ((), ()))


def mm(left, right, dims=NN):
    return lax.dot_general(left, right, dims, preferred_element_type=F32)


def swap(values, axis_name, bit):
    size = lax.axis_size(axis_name)
    return lax.ppermute(values, axis_name, [(i, i ^ bit) for i in range(size)])


def bits_of(axis_name):
    return [1 << i for i in range(lax.axis_size(axis_name).bit_length() - 1)]


def gather_bit(values, axis_name, bit, dim):
    other = swap(values, axis_name, bit)
    high = (lax.axis_index(axis_name) & bit) != 0
    return jnp.where(
        high, jnp.stack([other, values], axis=dim), jnp.stack([values, other], axis=dim)
    )


def gather_rows(block):
    rows, width = block.shape
    expert_bits, hidden_bits = bits_of("expert"), bits_of("hidden")
    for bit in expert_bits[1:]:
        block = gather_bit(block, "expert", bit, 0)
    block = block.reshape(-1, rows, width)
    outer = block.shape[0]
    half = width // 2 // 128 * 128
    up = block[:, :, :half]
    for bit in hidden_bits:
        up = gather_bit(up, "hidden", bit, 1)
    up = up.reshape(outer, -1, rows, half)
    down = block[:, :, half:]
    for step, bit in enumerate(reversed(hidden_bits)):
        down = gather_bit(down, "hidden", bit, 1 + step)
    down = down.reshape(outer, -1, rows, width - half)
    block = jnp.concatenate([up, down], axis=3)
    block = gather_bit(block, "expert", expert_bits[0], 1)
    return block.reshape(-1, width)


def pick(values, index, dim):
    return lax.dynamic_index_in_dim(values, index, dim, keepdims=False)


def reduce_bit(values, axis_name, bit, dim):
    mine = (lax.axis_index(axis_name) & bit) // bit
    other = swap(pick(values, 1 - mine, dim).astype(BF16), axis_name, bit)
    return pick(values, mine, dim) + other.astype(F32)


def reduce_rows(part, rows):
    width = part.shape[1]
    expert_bits, hidden_bits = bits_of("expert"), bits_of("hidden")
    n_outer = 1 << (len(expert_bits) - 1)
    part = part.reshape(n_outer, 2, -1, width)
    part = reduce_bit(part, "expert", expert_bits[0], 1)
    half = width // 2 // 128 * 128
    up = part[:, :, :half]
    for bit in reversed(hidden_bits):
        up = reduce_bit(up.reshape(n_outer, 2, -1, half), "hidden", bit, 1)
    down = part[:, :, half:]
    for step, bit in enumerate(hidden_bits):
        lead = 1 << (len(hidden_bits) - 1 - step)
        down = reduce_bit(
            down.reshape(n_outer, lead, 2, -1, width - half), "hidden", bit, 2
        )
    part = jnp.concatenate(
        [up.reshape(n_outer, rows, half), down.reshape(n_outer, rows, width - half)], axis=2
    )
    for bit in reversed(expert_bits[1:]):
        part = reduce_bit(part.reshape(2, -1, rows, width), "expert", bit, 0)
    return part.reshape(rows, width)


def spread_hidden(rows_own):
    half = rows_own.shape[0] // 2
    hidden_bits = bits_of("hidden")
    up, down = rows_own[:half], rows_own[half:]
    for bit in hidden_bits:
        up = jnp.concatenate([up, swap(up, "hidden", bit)], axis=0)
    for bit in reversed(hidden_bits):
        down = jnp.concatenate([down, swap(down, "hidden", bit)], axis=0)
    return jnp.concatenate([up, down], axis=0)


def collect_hidden(part_rows):
    half = part_rows.shape[0] // 2
    hidden_bits = bits_of("hidden")
    up, down = part_rows[:half], part_rows[half:]
    for bit in reversed(hidden_bits):
        size = up.shape[0] // 2
        up = up[:size].astype(F32) + swap(up[size:], "hidden", bit).astype(F32)
        up = up.astype(BF16)
    for bit in hidden_bits:
        size = down.shape[0] // 2
        down = down[:size].astype(F32) + swap(down[size:], "hidden", bit).astype(F32)
        down = down.astype(BF16)
    return jnp.concatenate([up, down], axis=0)


def to_experts(slots):
    return lax.all_to_all(slots, "expert", split_axis=0, concat_axis=0, tiled=True)


def head_parts(values, first_lane):
    lane = lax.broadcasted_iota(jnp.int32, values.shape, 1)
    return jnp.where(lane // HEAD_DIM == first_lane, values, 0.0)


def spare_lane(shape, head):
    lane = lax.broadcasted_iota(jnp.int32, shape, 1)
    return lane == (HEAD_DIM if head == 0 else 0)


def masked_keys(keys, head, length):
    key_pos = lax.broadcasted_iota(jnp.int32, keys.shape, 0)
    bias = jnp.where(key_pos < length, 0.0, MASKED)
    return jnp.where(spare_lane(keys.shape, head), bias, head_parts(keys, head)).astype(BF16)


def masked_queries(queries, head):
    return jnp.where(
        spare_lane(queries.shape, head), 1.0, head_parts(queries, head)
    ).astype(BF16)


def attend_forward_kernel(block, length_ref, q_ref, k_ref, v_ref, o_ref, lse_ref):
    pair = pl.program_id(0)
    length = length_ref[0]
    seq_len = q_ref.shape[0]
    scale = HEAD_DIM**-0.5
    queries = q_ref[...].astype(F32) * scale
    keys = k_ref[...].astype(F32)
    values = v_ref[...].astype(F32)

    @pl.when(pair == 0)
    def _():
        lse_ref[...] = jnp.zeros_like(lse_ref)

    heads = [
        (
            masked_queries(queries, head),
            masked_keys(keys, head, length),
            head_parts(values, head).astype(BF16),
        )
        for head in range(2)
    ]
    lane = lax.broadcasted_iota(jnp.int32, (block, 128), 1)
    on_diag = lax.broadcasted_iota(jnp.int32, (block, block), 0) >= lax.broadcasted_iota(
        jnp.int32, (block, block), 1
    )
    for index in range(seq_len // block):
        low, high = index * block, (index + 1) * block
        total = jnp.zeros((block, 128), F32)
        stats = lse_ref[low:high]
        for head in range(2):
            q_head, k_head, v_head = heads[head]
            diag = jnp.where(on_diag, mm(q_head[low:high], k_head[low:high], NT), MASKED)
            peak = jnp.max(diag, axis=1, keepdims=True)
            if index:
                past = mm(q_head[low:high], k_head[:low], NT)
                peak = jnp.maximum(peak, jnp.max(past, axis=1, keepdims=True))
            diag = jnp.exp(diag - peak)
            row_sum = jnp.sum(diag, axis=1, keepdims=True)
            mixed = mm(diag.astype(BF16), v_head[low:high])
            if index:
                past = jnp.exp(past - peak)
                row_sum = row_sum + jnp.sum(past, axis=1, keepdims=True)
                mixed = mixed + mm(past.astype(BF16), v_head[:low])
            total = total + mixed / row_sum
            stats = jnp.where(lane == 2 * pair + head, peak + jnp.log(row_sum), stats)
        o_ref[low:high] = total.astype(BF16)
        lse_ref[low:high] = stats


def attend_forward(qkv_rows, length, block):
    tok, width = qkv_rows.shape
    pairs = width // 3 // 128
    column = lambda offset: pl.BlockSpec((tok, 128), lambda i: (0, i + offset))
    return pl.pallas_call(
        functools.partial(attend_forward_kernel, block),
        grid=(pairs,),
        in_specs=[
            pl.BlockSpec(memory_space=pltpu.SMEM),
            column(0),
            column(pairs),
            column(2 * pairs),
        ],
        out_specs=[column(0), pl.BlockSpec((tok, 128), lambda i: (0, 0))],
        out_shape=[
            jax.ShapeDtypeStruct((tok, pairs * 128), BF16),
            jax.ShapeDtypeStruct((tok, 128), F32),
        ],
        name="attend_forward",
    )(length, qkv_rows, qkv_rows, qkv_rows)


def attend_backward_kernel(
    block, length_ref, q_ref, k_ref, v_ref, g_ref, lse_ref, dot_ref, dq_ref, dk_ref, dv_ref,
    dk_acc, dv_acc
):
    length = length_ref[0]
    seq_len = q_ref.shape[0]
    scale = HEAD_DIM**-0.5
    queries = q_ref[...].astype(F32) * scale
    keys = k_ref[...].astype(F32)
    grads = g_ref[...].astype(F32)
    values = v_ref[...]
    heads = [
        (
            masked_queries(queries, head),
            masked_keys(keys, head, length),
            head_parts(queries, head).astype(BF16),
            head_parts(keys * scale, head).astype(BF16),
            head_parts(grads, head).astype(BF16),
        )
        for head in range(2)
    ]
    on_diag = lax.broadcasted_iota(jnp.int32, (block, block), 0) <= lax.broadcasted_iota(
        jnp.int32, (block, block), 1
    )
    dk_acc[...] = jnp.zeros_like(dk_acc)
    dv_acc[...] = jnp.zeros_like(dv_acc)
    for index in range(seq_len // block):
        low, high = index * block, (index + 1) * block
        grad_q = jnp.zeros((block, 128), F32)
        for head in range(2):
            q_aug, k_aug, q_head, k_head, g_head = heads[head]
            lse = lse_ref[0, head : head + 1, low:high]
            row_dot = dot_ref[0, head : head + 1, low:high]
            for start, stop in ((0, low), (low, high)):
                if start == stop:
                    continue
                scores = mm(k_aug[start:stop], q_aug[low:high], NT)
                probs = jnp.exp(scores - lse)
                if start == low:
                    probs = jnp.where(on_diag, probs, 0.0)
                grad_p = mm(values[start:stop], g_head[low:high], NT)
                grad_s = (probs * (grad_p - row_dot)).astype(BF16)
                dv_acc[start:stop] += mm(probs.astype(BF16), g_head[low:high])
                dk_acc[start:stop] += mm(grad_s, q_head[low:high])
                grad_q = grad_q + mm(grad_s, k_head[start:stop], TN)
        dq_ref[low:high] = grad_q.astype(BF16)
    dk_ref[...] = dk_acc[...].astype(BF16)
    dv_ref[...] = dv_acc[...].astype(BF16)


def attend_backward(qkv_rows, grad_mixed, lse, row_dot, length, block):
    tok, width = qkv_rows.shape
    pairs = width // 3 // 128
    column = lambda offset: pl.BlockSpec((tok, 128), lambda i: (0, i + offset))
    row = pl.BlockSpec((1, 2, tok), lambda i: (i, 0, 0))
    return pl.pallas_call(
        functools.partial(attend_backward_kernel, block),
        grid=(pairs,),
        in_specs=[
            pl.BlockSpec(memory_space=pltpu.SMEM),
            column(0),
            column(pairs),
            column(2 * pairs),
            column(0),
            row,
            row,
        ],
        out_specs=[column(0)] * 3,
        out_shape=[jax.ShapeDtypeStruct((tok, pairs * 128), BF16)] * 3,
        scratch_shapes=[pltpu.VMEM((tok, 128), F32)] * 2,
        name="attend_backward",
    )(length, qkv_rows, qkv_rows, qkv_rows, grad_mixed, lse, row_dot)


def layer_norm(values, gain_row, shift_row):
    row_mean = jnp.mean(values, axis=-1, keepdims=True)
    centered = values - row_mean
    inverse = lax.rsqrt(jnp.mean(centered * centered, axis=-1, keepdims=True) + EPSILON)
    normed = centered * inverse
    return (normed * gain_row + shift_row, normed, inverse)


def norm_back(grad_rows, normed, inverse, gain_row):
    scaled = grad_rows * gain_row
    first_mean = jnp.mean(scaled, axis=-1, keepdims=True)
    second_mean = jnp.mean(scaled * normed, axis=-1, keepdims=True)
    grad_in = inverse * (scaled - first_mean - normed * second_mean)
    return (grad_in, jnp.sum(grad_rows * normed, axis=0), jnp.sum(grad_rows, axis=0))


def nesterov(master, momentum, average, grad_full, rate):
    moment_new = MOMENT * momentum + grad_full
    weight_new = master - rate * (grad_full + MOMENT * moment_new)
    return (grad_full, moment_new, weight_new, KEEP_MEAN * average + (1.0 - KEEP_MEAN) * weight_new)


def per_device(
    inputs,
    out_grad,
    seq_lengths,
    routes,
    norm_master,
    norm_momentum,
    norm_average,
    qkv_master,
    qkv_momentum,
    qkv_average,
    proj_master,
    proj_momentum,
    proj_average,
    router_master,
    router_momentum,
    router_average,
    frozen_in,
    frozen_out,
    expert_in_master,
    expert_in_momentum,
    expert_in_average,
    expert_out_master,
    expert_out_momentum,
    expert_out_average,
):
    tok_dev, model_width = inputs.shape
    seq_dev = seq_lengths.shape[0]
    assert seq_dev == 1
    n_expert = lax.axis_size("expert")
    n_hidden = lax.axis_size("hidden")
    experts = 2 * n_expert
    capacity = tok_dev * 2 // experts // 2
    slot_count = experts * capacity
    tokens_all = tok_dev * n_expert * n_hidden
    own_rows = model_width // (n_expert * n_hidden)
    block_rows = min(256, tok_dev)
    expert_index = lax.axis_index("expert")

    pad_norm = 128 - 4
    first_block = jnp.concatenate(
        [qkv_master, norm_master.T, jnp.zeros((own_rows, pad_norm), F32)], axis=1
    ).astype(BF16)
    pad_router = 128 - experts
    second_block = jnp.concatenate(
        [proj_master.T, router_master, jnp.zeros((own_rows, pad_router), F32)], axis=1
    ).astype(BF16)
    first_full = gather_rows(first_block)
    qkv_full = first_full[:, : 3 * model_width]
    norm_full = first_full[:, 3 * model_width :].astype(F32).T
    second_full = gather_rows(second_block)
    proj_full = second_full[:, :model_width]
    router_full = second_full[:, model_width:]

    row_ids = jnp.arange(tok_dev, dtype=jnp.int32)
    live_rows = row_ids < seq_lengths[0]
    live_float = live_rows.astype(F32)[:, None]
    expert_ids = jnp.arange(128, dtype=jnp.int32)
    match = [routes[:, k : k + 1] == expert_ids[None, :] for k in range(2)]
    counts = ((match[0] | match[1]) & live_rows[:, None]).astype(BF16)
    earlier = (row_ids[:, None] > row_ids[None, :]).astype(BF16)
    before = mm(earlier, counts)
    slot_ids = jnp.arange(slot_count, dtype=jnp.int32)
    chosen = None
    for k in range(2):
        rank = jnp.sum(jnp.where(match[k], before, 0.0), axis=1).astype(jnp.int32)
        kept = live_rows & (rank < capacity)
        expert_of = routes[:, k]
        slot = (expert_of % 2 * n_expert + expert_of // 2) * capacity + rank
        hit = jnp.where(kept, slot, -1)[:, None] == slot_ids[None, :]
        chosen = hit if chosen is None else chosen | hit
    select = chosen.astype(BF16)

    route_part = jnp.concatenate(
        [routes.astype(BF16), jnp.zeros((tok_dev, 126), BF16)], axis=1
    )
    grad_out_rows = jnp.where(live_rows[:, None], out_grad, jnp.zeros_like(out_grad))
    early = jnp.concatenate([grad_out_rows, route_part], axis=1)
    early_slots = mm(select, early, TN).astype(BF16)
    early_slots = early_slots.reshape(2, n_expert, capacity, model_width + 128)
    weight_in = (frozen_in[0], expert_in_master[0].astype(BF16))
    weight_out = (frozen_out[0], expert_out_master[0].astype(BF16))
    grad_rows, back_hidden = [], []
    for part in range(2):
        group = spread_hidden(to_experts(early_slots[part]).reshape(-1, model_width + 128))
        grad_rows.append(group)
        back_hidden.append(mm(group[:, :model_width], weight_out[part], NT))

    resid_in = inputs.astype(F32)
    normed_one, base_one, inverse_one = layer_norm(resid_in, norm_full[0], norm_full[1])
    attn_in = normed_one.astype(BF16)
    qkv_rows = mm(attn_in, qkv_full).astype(BF16)
    attn_out, log_totals = attend_forward(qkv_rows, seq_lengths, block_rows)
    resid_mid = resid_in + mm(attn_out, proj_full, NT)
    normed_two, base_two, inverse_two = layer_norm(resid_mid, norm_full[2], norm_full[3])
    moe_in = normed_two.astype(BF16)

    moe_slots = mm(select, moe_in, TN).astype(BF16).reshape(2, n_expert, capacity, model_width)
    returned, value_parts, router_part = [], [], 0.0
    weight_grads = None
    for part in range(2):
        rows = spread_hidden(to_experts(moe_slots[part]).reshape(-1, model_width))
        group = grad_rows[part]
        own = 2 * expert_index + part
        route_sum = group[:, model_width].astype(F32) + group[:, model_width + 1].astype(F32)
        other = route_sum.astype(jnp.int32) - own
        is_own = (expert_ids == own).astype(F32)[None, :]
        signs = is_own - (other[:, None] == expert_ids[None, :]).astype(F32)
        gap = jnp.sum(mm(rows, router_full) * signs, axis=1, keepdims=True)
        gate = jax.nn.sigmoid(gap)
        pre_act = mm(rows, weight_in[part])
        root = math.sqrt(2.0 / math.pi)
        squared = pre_act * pre_act
        curve = jnp.tanh(root * pre_act * (1.0 + 0.044715 * squared))
        activation = (0.5 * pre_act * (1.0 + curve)).astype(BF16)
        slope = 0.5 * (1.0 + curve) + 0.5 * pre_act * (1.0 - curve * curve) * root * (
            1.0 + 3 * 0.044715 * squared
        )
        back = back_hidden[part]
        grad_pre = (slope * (gate * back)).astype(BF16)
        grad_gate = jnp.sum(activation.astype(F32) * back, axis=1, keepdims=True)
        grad_logit = (gate * (1.0 - gate) * grad_gate * signs).astype(BF16)
        grad_in = (mm(grad_pre, weight_in[part], NT) + mm(grad_logit, router_full, NT)).astype(BF16)
        returned.append(to_experts(collect_hidden(grad_in).reshape(n_expert, capacity, model_width)))
        value_parts.append((gate * mm(activation, weight_out[part])).astype(BF16))
        router_part = router_part + mm(rows, grad_logit, TN)
        if part == 1:
            pair_grad = (gate * group[:, :model_width].astype(F32)).astype(BF16)
            weight_grads = (mm(rows, grad_pre, TN), mm(activation, pair_grad, TN))

    back_slots = jnp.concatenate(returned, axis=0).reshape(slot_count, model_width)
    grad_norm_two = mm(select, back_slots)
    grad_out = grad_out_rows.astype(F32)
    grad_low_two, gain_two_grad, shift_two_grad = norm_back(
        grad_norm_two, base_two, inverse_two, norm_full[2]
    )
    grad_mid = grad_out + grad_low_two
    grad_branch = grad_mid.astype(BF16)
    grad_attn = mm(grad_branch, proj_full).astype(BF16)

    value_slots = jnp.concatenate(
        [
            to_experts(collect_hidden(rows).reshape(n_expert, capacity, model_width))
            for rows in value_parts
        ],
        axis=0,
    ).reshape(slot_count, model_width)
    outputs = (live_float * (resid_mid + mm(select, value_slots))).astype(BF16)

    head_of = jnp.arange(model_width, dtype=jnp.int32) // HEAD_DIM
    head_sums = (head_of[None, :] == jnp.arange(HEADS, dtype=jnp.int32)[:, None]).astype(F32)
    row_dot = lax.dot_general(
        head_sums,
        grad_attn.astype(F32) * attn_out.astype(F32),
        NT,
        precision=lax.Precision.HIGHEST,
        preferred_element_type=F32,
    ).reshape(HEADS // 2, 2, tok_dev)
    log_rows = log_totals.T[:HEADS].reshape(HEADS // 2, 2, tok_dev)
    grad_q, grad_k, grad_v = attend_backward(
        qkv_rows, grad_attn, log_rows, row_dot, seq_lengths, block_rows
    )
    grad_qkv = jnp.concatenate([grad_q, grad_k, grad_v], axis=1)
    qkv_part = mm(attn_in, grad_qkv, TN)
    grad_norm_one = mm(grad_qkv, qkv_full, NT)
    grad_low_one, gain_one_grad, shift_one_grad = norm_back(
        grad_norm_one, base_one, inverse_one, norm_full[0]
    )
    input_grad = grad_mid + grad_low_one

    proj_part = mm(grad_branch, attn_out, TN)
    early_sums = reduce_rows(jnp.concatenate([proj_part, router_part], axis=1), own_rows)
    proj_sum = early_sums[:, :model_width].T
    router_sum = early_sums[:, model_width : model_width + experts]
    norm_part = jnp.stack([gain_one_grad, shift_one_grad, gain_two_grad, shift_two_grad], axis=1)
    norm_part = jnp.concatenate([norm_part, jnp.zeros((model_width, 124), F32)], axis=1)
    late_sums = reduce_rows(jnp.concatenate([qkv_part, norm_part], axis=1), own_rows)
    qkv_sum = late_sums[:, : 3 * model_width]
    norm_sum = late_sums[:, 3 * model_width : 3 * model_width + 4].T

    norm_rate = 0.1 / math.sqrt(tokens_all)
    qkv_rate = 1.0 / math.sqrt(model_width * tokens_all)
    proj_rate = 40.0 / math.sqrt(model_width * tokens_all)
    router_rate = 0.08 * math.sqrt(experts / (model_width * tokens_all))
    in_rate = 5.0 * math.sqrt(experts / (model_width * tokens_all))
    out_rate = 2.5 * math.sqrt(experts / (FF * tokens_all))
    norm_set = nesterov(norm_master, norm_momentum, norm_average, norm_sum, norm_rate)
    qkv_set = nesterov(qkv_master, qkv_momentum, qkv_average, qkv_sum, qkv_rate)
    proj_set = nesterov(proj_master, proj_momentum, proj_average, proj_sum, proj_rate)
    router_set = nesterov(router_master, router_momentum, router_average, router_sum, router_rate)
    in_set = nesterov(
        expert_in_master, expert_in_momentum, expert_in_average, weight_grads[0][None], in_rate
    )
    out_set = nesterov(
        expert_out_master, expert_out_momentum, expert_out_average, weight_grads[1][None], out_rate
    )
    return (
        outputs,
        input_grad,
        *norm_set,
        *qkv_set,
        *proj_set,
        *router_set,
        *in_set,
        *out_set,
    )


def solution(mesh):
    rows = P(("expert", "hidden"), None)
    columns = P(None, ("expert", "hidden"))
    expert_in = P("expert", None, "hidden")
    expert_out = P("expert", "hidden", None)
    return jax.shard_map(
        per_device,
        mesh=mesh,
        in_specs=(
            rows,
            rows,
            P(("expert", "hidden")),
            rows,
            *[columns] * 3,
            *[rows] * 3,
            *[columns] * 3,
            *[rows] * 3,
            expert_in,
            expert_out,
            *[expert_in] * 3,
            *[expert_out] * 3,
        ),
        out_specs=(
            rows,
            rows,
            *[columns] * 4,
            *[rows] * 4,
            *[columns] * 4,
            *[rows] * 4,
            *[expert_in] * 4,
            *[expert_out] * 4,
        ),
        check_vma=False,
    )
```

time: 1340 us -> 678 us (0.51)
  blocking collectives: 277 us -> 0 us
  waiting for transfers between devices: 427 us -> 164 us
  matrix products: 267 us -> 122 us
  starting transfers between devices: 9.55 us -> 105 us
  other arithmetic: 157 us -> 80.7 us
  Pallas kernels: 0 us -> 55.2 us
  local copies, waits for them, and re-layouts: 171 us -> 138 us
    reduce_scatter x4 -> x0, waiting for transfers between devices: 282 us -> none  [the longest x1 121 us: per_device(): lax.psum_scatter(jnp.einsum('rlf,lfd->rld', piece_rows, weight_out, prefe...]
    all_gather x2 -> x0, blocking collectives: 158 us -> none  [the longest x1 88.4 us: per_device(): lax.all_gather(router_master.astype(jnp.bfloat16), ('expert', 'hidden'),...]
    ppermute x0 -> x60, waiting for transfers between devices: none -> 158 us  [swap(): return lax.ppermute(values, axis_name, [(i, i ^ bit) for i in range(size)])]
    dot_general x29 -> x28, matrix products: 267 us -> 122 us  [the longest x27 119 us: mm(): return lax.dot_general(left, right, dims, preferred_element_type=F32)]
    all_gather x4 -> x0, waiting for transfers between devices: 125 us -> none  [the longest x1 67.9 us: per_device(): grad_group = lax.all_gather(grad_slots, 'hidden', axis=0, tiled=True)]
    all_to_all x2 -> x0, blocking collectives: 80.5 us -> none  [the longest x1 40.3 us: per_device(): lax.all_to_all(send_rows, 'expert', split_axis=0, concat_axis=0, tiled=True)]
    ppermute x0 -> x60, starting transfers between devices: none -> 67.5 us  [swap(): return lax.ppermute(values, axis_name, [(i, i ^ bit) for i in range(size)])]
    reduce_sum x9 -> x2, other arithmetic: 71.6 us -> 8.09 us  [norm_back(): jnp.sum(grad_rows * normed, axis=0)]
  transfers between devices with their start and end apart: 10 -> 68, of which waited for: 6 -> 35; matrix products, arithmetic and copies ran while one was open for 30% -> 42% of each run, Pallas kernels for 0% -> 8%
where the time goes in v1:
time: 678 us; the launch traced here: 669 us
  waiting for transfers between devices  164 us (24%)
  local copies, waits for them, and re-layouts  138 us (20%)
  matrix products  122 us (18%)
  starting transfers between devices  105 us (15%)
  other arithmetic  80.7 us (12%)
  Pallas kernels  55.2 us (8%)
    ppermute x60, waiting for transfers between devices, swap(): return lax.ppermute(values, axis_name, [(i, i ^ bit) for i in range(size)])  158 us
    dot_general x27, matrix products, mm(): return lax.dot_general(left, right, dims, preferred_element_type=F32)  119 us
    ppermute x60, starting transfers between devices, swap(): return lax.ppermute(values, axis_name, [(i, i ^ bit) for i in range(size)])  67.5 us
    unnamed x230, local copies, waits for them, and re-layouts  57.8 us
    all_to_all x8, starting transfers between devices, to_experts(): lax.all_to_all(slots, 'expert', split_axis=0, concat_axis=0, tiled=True)  38 us
    pallas_call x1, Pallas kernels, attend_backward(): pl.pallas_call(functools.partial(attend_backward_kernel, block), grid=(pa...  31.9 us
    pallas_call x1, Pallas kernels, attend_forward(): pl.pallas_call(functools.partial(attend_forward_kernel, block), grid=(pai...  23.2 us
    concatenate x10, local copies, waits for them, and re-layouts, per_device(): jnp.concatenate([qkv_part, norm_part], axis=1)  22.7 us
  transfers between devices with their start and end apart: 68, of which 35 were waited for; matrix products, arithmetic and copies ran while one was open for 42% of the time, Pallas kernels for 8%

profile of v1, /device:TPU:0, one launch (start us, length us, event | category | flops | bytes accessed | tf_op | source)
XLA Modules:
  0.0 668.8 jit_solution(17884506063634614888)
XLA Ops:
  17.6 5.3 all-to-all-start.4
  32.3 23.6 %collective-permute-done.8 = bf16[2,24,896]{2,1,0:T(8,128)(2,1)S(1)} collective-permute-done((bf16[2,24,896]{2,1,0:T(8,128)(2,1)S(1)}, bf16[2,24,896]{2,1,0:T(8,128)(2,1)S(1)}, u32[]{:S(2)}, u32[]{:S(2)}) %collective-permute-start.8) | collective-permute-done | bytes 86048 | tf_op jit(solution)/shard_map/ppermute | solution.py:34
  75.6 5.5 collective-permute-done.3
  83.8 4.5 all-to-all-start.1
  147.2 5.9 convolution_convert_fusion.q_ref.k_ref.v_ref
  153.2 23.2 %attend_forward.1 = (bf16[1024,768]{1,0:T(8,128)(2,1)}, f32[1024,128]{1,0:T(8,128)}) custom-call(s32[1]{0:T(128)} %copy.398.length_ref, bf16[1024,2304]{1,0:T(8,128)(2,1)} %convolution_convert_fusion.q_ref.k_ref.v_ref, bf16[1024,2304]{1,0:T(8,128)(2,1)} %convolution_convert_fusion.q_ref.k_ref.v_ref, bf16[1024,2304]{1,0:T(8,128)(2,1)} %convolution_convert_fusion.q_ref.k_ref.v_ref), custom_call_target="tpu_custom_call" | custom-call | tf_op jit(solution)/shard_map/attend_forward/pallas_call | solution.py:209
  209.9 5.3 collective-permute-done.33
  216.2 5.0 all-to-all-start
  223.1 11.3 %collective-permute-done.21 = bf16[512,896]{0,1:T(8,128)(2,1)} collective-permute-done((bf16[512,896]{0,1:T(8,128)(2,1)}, bf16[512,896]{0,1:T(8,128)(2,1)}, u32[]{:S(2)}, u32[]{:S(2)}) %collective-permute-start.21) | collective-permute-done | bytes 917536 | tf_op jit(solution)/shard_map/ppermute | solution.py:34
  244.6 6.2 collective-permute-done.26
  253.9 5.3 collective-permute-done.14
  262.4 15.3 %collective-permute-done.27 = bf16[512,768]{1,0:T(8,128)(2,1)S(1)} collective-permute-done((bf16[512,768]{1,0:T(8,128)(2,1)S(1)}, bf16[512,768]{1,0:T(8,128)(2,1)S(1)}, u32[]{:S(2)}, u32[]{:S(2)}) %collective-permute-start.27) | collective-permute-done | bytes 786464 | tf_op jit(solution)/shard_map/ppermute | solution.py:34
  282.3 10.2 %multiply_reduce_fusion = (f32[2048]{0:T(1024)S(1)}, bf16[2048,768]{0,1:T(8,128)(2,1)}) fusion(f32[2048,768]{0,1:T(8,128)S(1)} %fusion.64, f32[2048]{0:T(1024)S(1)} %add_divide_fusion, bf16[2048,896]{0,1:T(8,128)(2,1)} %constant_dynamic-update-slice_fusion.18, f32[1,768,768]{2,1,0:T(8,128)S(1)} %copy-done.91), kind=kOutput, calls=%fused_computation.2 | convolution fusion | flops 2454255616 | bytes 14958592 | tf_op jit(solution)/shard_map/dot_general | solution.py:29
  294.1 6.0 multiply_convert_fusion.3
  300.2 4.7 fusion.69
  306.2 8.1 %multiply_reduce_fusion.1 = (f32[2048]{0:T(1024)S(1)}, f32[2048,768]{0,1:T(8,128)}) fusion(f32[2048,768]{0,1:T(8,128)} %fusion.69, bf16[2048,896]{0,1:T(8,128)(2,1)} %constant_dynamic-update-slice_fusion.6, bf16[1,768,768]{2,1,0:T(8,128)(2,1)S(1)} %copy-done), kind=kOutput, calls=%fused_computation.5 | convolution fusion | flops 2434791424 | bytes 16916480 | tf_op jit(solution)/shard_map/dot_general | solution.py:29
  314.3 9.2 %fusion.24 = f32[2048,768]{1,0:T(8,128)S(1)} fusion(f32[2048,768]{0,1:T(8,128)} %get-tuple-element.283, f32[2048,768]{0,1:T(8,128)} %fusion.69, f32[2048]{0:T(1024)S(1)} %get-tuple-element.275, bf16[1,768,768]{2,1,0:T(8,128)(2,1)S(1)} %copy-done.92), kind=kOutput, calls=%fused_computation.53 | convolution fusion | flops 2445803520 | bytes 20062208 | tf_op jit(solution)/shard_map/dot_general | solution.py:29
  335.7 7.9 %multiply_add_fusion.3 = (f32[1,768,768]{2,1,0:T(8,128)}, f32[1,768,768]{2,1,0:T(8,128)}, f32[1,768,768]{2,1,0:T(8,128)}, f32[1,768,768]{2,1,0:T(8,128)}) fusion(f32[1,768,768]{2,1,0:T(8,128)S(1)} %copy-done.89, f32[1,768,768]{2,1,0:T(8,128)S(1)} %copy-done.88, f32[1,768,768]{2,1,0:T(8,128)S(1)} %copy-done.90, ...), kind=kOutput, calls=%fused_computation.74 | convolution fusion | flops 2421227520 | bytes 22806528 | tf_op jit(solution)/shard_map/dot_general | solution.py:29
  343.7 13.1 %multiply_add_fusion.1 = (f32[1,768,768]{2,1,0:T(8,128)}, f32[1,768,768]{2,1,0:T(8,128)}, f32[1,768,768]{2,1,0:T(8,128)}, f32[1,768,768]{2,1,0:T(8,128)}) fusion(f32[1,768,768]{2,1,0:T(8,128)} %param.47, f32[1,768,768]{2,1,0:T(8,128)S(1)} %copy-done.91, f32[1,768,768]{2,1,0:T(8,128)} %param.46, f32[2048]{0:T(1024)S(1)} %add_divide_fusion, ...), kind=kOutput, calls=%fused_computation.71 | convolution fusion | flops 2440101888 | bytes 25960448 | tf_op jit(solution)/shard_map/dot_general | solution.py:29
  356.8 5.9 multiply_convert_fusion.5
  374.2 17.7 %collective-permute-done.41 = bf16[256,768]{1,0:T(8,128)(2,1)S(1)} collective-permute-done((bf16[256,768]{1,0:T(8,128)(2,1)S(1)}, bf16[256,768]{1,0:T(8,128)(2,1)S(1)}, u32[]{:S(2)}, u32[]{:S(2)}) %collective-permute-start.41) | collective-permute-done | bytes 393248 | tf_op jit(solution)/shard_map/ppermute | solution.py:34
  393.5 4.8 all-to-all-start.6
  424.5 4.9 collective-permute-done.36
  441.4 4.5 collective-permute-done.35
  449.5 4.7 all-to-all-start.2
  463.6 4.6 multiply_reduce_fusion.2
  485.3 31.9 %attend_backward.1 = (bf16[1024,768]{1,0:T(8,128)(2,1)}, bf16[1024,768]{1,0:T(8,128)(2,1)}, bf16[1024,768]{1,0:T(8,128)(2,1)}) custom-call(s32[1]{0:T(128)} %copy.398.length_ref, bf16[1024,2304]{1,0:T(8,128)(2,1)} %convolution_convert_fusion.q_ref.k_ref.v_ref, bf16[1024,2304]{1,0:T(8,128)(2,1)} %convolution_convert_fusion.q_ref.k_ref.v_ref, ...), custom_call_target="tpu_custom_call" | custom-call | tf_op jit(solution)/shard_map/attend_backward/pallas_call | solution.py:282
  528.1 5.0 all-to-all-start.5
  533.2 9.5 %fusion.161 = (f32[768]{0:T(1024)}, f32[1024,768]{1,0:T(8,128)}) fusion(bf16[1024,2304]{1,0:T(8,128)(2,1)} %copy-done.38, bf16[768,2432]{1,0:T(8,128)(2,1)} %bitcast.223), kind=kOutput, calls=%fused_computation.381 | convolution fusion | flops 3624664320 | bytes 11406336 | tf_op jit(solution)/shard_map/dot_general | solution.py:29
  561.1 8.9 %concatenate.276 = f32[4,2,96,2432]{3,2,0,1:T(8,128)} concatenate(f32[4,2,96,2304]{3,2,0,1:T(8,128)} %copy.340, f32[4,2,96,1]{3,2,0,1:T(8,128)S(1)} %copy.341, f32[4,2,96,1]{3,2,0,1:T(8,128)} %copy.342, f32[4,2,96,1]{3,2,0,1:T(8,128)} %copy.343, f32[4,2,96,1]{3,2,0,1:T(8,128)} %copy.344, f32[4,2,96,124]{3,2,0,1:T(8,128)} %broadcast_in_dim.42), dimensions={3} | concatenate | bytes 14942208 | tf_op jit(solution)/shard_map/concatenate | solution.py:499
  616.3 5.6 collective-permute-done.47
  654.0 4.5 multiply_add_fusion.5
  (560 shorter events, 376.7 us)
Async XLA Ops:
  17.6 66.1 %all-to-all-start.4 = ((bf16[8,64,896]{2,1,0:T(8,128)(2,1)}), bf16[8,64,896]{2,1,0:T(8,128)(2,1)}, u32[]{:S(2)}, u32[]{:S(2)}) async-start(bf16[8,64,896]{2,1,0:T(8,128)(2,1)} %bitcast.228), calls=%async_computation.4 | async-start | bytes 1835008 | tf_op jit(solution)/shard_map/all_to_all | solution.py:131
  28.3 27.7 %collective-permute-start.8 = (bf16[2,24,896]{2,1,0:T(8,128)(2,1)S(1)}, bf16[2,24,896]{2,1,0:T(8,128)(2,1)S(1)}, u32[]{:S(2)}, u32[]{:S(2)}) collective-permute-start(bf16[2,24,896]{2,1,0:T(8,128)(2,1)S(1)} %maximum_select_fusion.18), channel_id=1, source_target_pairs={{0,16},{4,20},{8,24},{12,28},{16,0},{20,4},{24,8},{28,12},{1,17},{... | collective-permute-start | bytes 258056 | tf_op jit(solution)/shard_map/ppermute | solution.py:34
  32.2 31.1 %collective-permute-start.1 = (bf16[2,24,2432]{2,1,0:T(8,128)(2,1)S(1)}, bf16[2,24,2432]{2,1,0:T(8,128)(2,1)S(1)}, u32[]{:S(2)}, u32[]{:S(2)}) collective-permute-start(bf16[2,24,2432]{2,1,0:T(8,128)(2,1)S(1)} %maximum_select_fusion.11), channel_id=1, source_target_pairs={{0,16},{4,20},{8,24},{12,28},{16,0},{20,4},{24,8},{28,12},{1,17},{... | collective-permute-start | bytes 700424 | tf_op jit(solution)/shard_map/ppermute | solution.py:34
  58.2 35.6 %collective-permute-start.11 = (bf16[4,24,512]{2,1,0:T(8,128)(2,1)}, bf16[4,24,512]{2,1,0:T(8,128)(2,1)}, u32[]{:S(2)}, u32[]{:S(2)}) collective-permute-start(bf16[4,24,512]{2,1,0:T(8,128)(2,1)} %get-tuple-element.269), channel_id=1, source_target_pairs={{0,2},{1,3},{2,0},{3,1},{4,6},{5,7},{6,4},{7,5},{8,10},{9,11},{10,... | collective-permute-start | bytes 294920 | tf_op jit(solution)/shard_map/ppermute | solution.py:34
  61.1 36.2 %collective-permute-start.10 = (bf16[4,2,24,384]{3,2,0,1:T(8,128)(2,1)}, bf16[4,2,24,384]{3,2,0,1:T(8,128)(2,1)}, u32[]{:S(2)}, u32[]{:S(2)}) collective-permute-start(bf16[4,2,24,384]{3,2,0,1:T(8,128)(2,1)} %maximum_select_fusion.16), channel_id=1, source_target_pairs={{0,2},{1,3},{2,0},{3,1},{4,6},{5,7},{6,4},{7,5},{8,10},{9,11},{10,... | collective-permute-start | bytes 442376 | tf_op jit(solution)/shard_map/ppermute | solution.py:34
  83.8 28.3 %all-to-all-start.1 = ((bf16[8,64,896]{2,1,0:T(8,128)(2,1)}), bf16[8,64,896]{2,1,0:T(8,128)(2,1)}, u32[]{:S(2)}, u32[]{:S(2)}) async-start(bf16[8,64,896]{2,1,0:T(8,128)(2,1)} %bitcast.227), calls=%async_computation.1 | async-start | bytes 1835008 | tf_op jit(solution)/shard_map/all_to_all | solution.py:131
  93.3 49.3 %collective-permute-start.6 = (bf16[4,4,24,2432]{3,2,1,0:T(8,128)(2,1)}, bf16[4,4,24,2432]{3,2,1,0:T(8,128)(2,1)}, u32[]{:S(2)}, u32[]{:S(2)}) collective-permute-start(bf16[4,4,24,2432]{3,2,1,0:T(8,128)(2,1)} %get-tuple-element.241), channel_id=1, source_target_pairs={{0,4},{4,0},{8,12},{12,8},{16,20},{20,16},{24,28},{28,24},{1,5},{5... | collective-permute-start | bytes 5603336 | tf_op jit(solution)/shard_map/ppermute | solution.py:34
  106.5 30.0 %collective-permute-start.30 = (bf16[256,896]{0,1:T(8,128)(2,1)}, bf16[256,896]{0,1:T(8,128)(2,1)}, u32[]{:S(2)}, u32[]{:S(2)}) collective-permute-start(bf16[256,896]{0,1:T(8,128)(2,1)} %copy.330), channel_id=1, source_target_pairs={{0,1},{1,0},{2,3},{3,2},{4,5},{5,4},{6,7},{7,6},{8,9},{9,8},{10,11... | collective-permute-start | bytes 1376264 | tf_op jit(solution)/shard_map/ppermute | solution.py:34
  130.6 59.1 %collective-permute-start.32 = (bf16[256,896]{0,1:T(8,128)(2,1)}, bf16[256,896]{0,1:T(8,128)(2,1)}, u32[]{:S(2)}, u32[]{:S(2)}) collective-permute-start(bf16[256,896]{0,1:T(8,128)(2,1)} %copy.331), channel_id=1, source_target_pairs={{0,2},{1,3},{2,0},{3,1},{4,6},{5,7},{6,4},{7,5},{8,10},{9,11},{10,... | collective-permute-start | bytes 1376264 | tf_op jit(solution)/shard_map/ppermute | solution.py:34
  133.1 59.5 %collective-permute-start.20 = (bf16[256,896]{0,1:T(8,128)(2,1)}, bf16[256,896]{0,1:T(8,128)(2,1)}, u32[]{:S(2)}, u32[]{:S(2)}) collective-permute-start(bf16[256,896]{0,1:T(8,128)(2,1)} %copy.323), channel_id=1, source_target_pairs={{0,2},{1,3},{2,0},{3,1},{4,6},{5,7},{6,4},{7,5},{8,10},{9,11},{10,... | collective-permute-start | bytes 1376264 | tf_op jit(solution)/shard_map/ppermute | solution.py:34
  138.6 63.3 %collective-permute-start.31 = (bf16[512,896]{0,1:T(8,128)(2,1)}, bf16[512,896]{0,1:T(8,128)(2,1)}, u32[]{:S(2)}, u32[]{:S(2)}) collective-permute-start(bf16[512,896]{0,1:T(8,128)(2,1)} %pad_maximum_fusion.6), channel_id=1, source_target_pairs={{0,2},{1,3},{2,0},{3,1},{4,6},{5,7},{6,4},{7,5},{8,10},{9,11},{10,... | collective-permute-start | bytes 2752520 | tf_op jit(solution)/shard_map/ppermute | solution.py:34
  141.2 63.8 %collective-permute-start.19 = (bf16[512,896]{0,1:T(8,128)(2,1)}, bf16[512,896]{0,1:T(8,128)(2,1)}, u32[]{:S(2)}, u32[]{:S(2)}) collective-permute-start(bf16[512,896]{0,1:T(8,128)(2,1)} %pad_maximum_fusion.4), channel_id=1, source_target_pairs={{0,2},{1,3},{2,0},{3,1},{4,6},{5,7},{6,4},{7,5},{8,10},{9,11},{10,... | collective-permute-start | bytes 2752520 | tf_op jit(solution)/shard_map/ppermute | solution.py:34
  184.7 31.6 %all-to-all-start.3 = ((bf16[8,64,768]{2,1,0:T(8,128)(2,1)}), bf16[8,64,768]{2,1,0:T(8,128)(2,1)}, u32[]{:S(2)}, u32[]{:S(2)}) async-start(bf16[8,64,768]{2,1,0:T(8,128)(2,1)} %bitcast.242), calls=%async_computation.3 | async-start | bytes 1572864 | tf_op jit(solution)/shard_map/all_to_all | solution.py:131
  194.5 39.9 %collective-permute-start.21 = (bf16[512,896]{0,1:T(8,128)(2,1)}, bf16[512,896]{0,1:T(8,128)(2,1)}, u32[]{:S(2)}, u32[]{:S(2)}) collective-permute-start(bf16[512,896]{0,1:T(8,128)(2,1)} %pad_maximum_fusion.5), channel_id=1, source_target_pairs={{0,1},{1,0},{2,3},{3,2},{4,5},{5,4},{6,7},{7,6},{8,9},{9,8},{10,11... | collective-permute-start | bytes 2752520 | tf_op jit(solution)/shard_map/ppermute | solution.py:34
  216.2 26.0 %all-to-all-start = ((bf16[8,64,768]{2,1,0:T(8,128)(2,1)}), bf16[8,64,768]{2,1,0:T(8,128)(2,1)S(1)}, u32[]{:S(2)}, u32[]{:S(2)}) async-start(bf16[8,64,768]{2,1,0:T(8,128)(2,1)} %bitcast.54), calls=%async_computation | async-start | bytes 1572864 | tf_op jit(solution)/shard_map/all_to_all | solution.py:131
  250.9 26.9 %collective-permute-start.27 = (bf16[512,768]{1,0:T(8,128)(2,1)S(1)}, bf16[512,768]{1,0:T(8,128)(2,1)S(1)}, u32[]{:S(2)}, u32[]{:S(2)}) collective-permute-start(bf16[512,768]{1,0:T(8,128)(2,1)S(1)} %pad_maximum_fusion.11), channel_id=1, source_target_pairs={{0,2},{1,3},{2,0},{3,1},{4,6},{5,7},{6,4},{7,5},{8,10},{9,11},{10,... | collective-permute-start | bytes 2359304 | tf_op jit(solution)/shard_map/ppermute | solution.py:34
  259.3 34.7 %collective-permute-start.15 = (bf16[512,768]{1,0:T(8,128)(2,1)S(1)}, bf16[512,768]{1,0:T(8,128)(2,1)S(1)}, u32[]{:S(2)}, u32[]{:S(2)}) collective-permute-start(bf16[512,768]{1,0:T(8,128)(2,1)S(1)} %pad_maximum_fusion.8), channel_id=1, source_target_pairs={{0,2},{1,3},{2,0},{3,1},{4,6},{5,7},{6,4},{7,5},{8,10},{9,11},{10,... | collective-permute-start | bytes 2359304 | tf_op jit(solution)/shard_map/ppermute | solution.py:34
  261.0 39.1 %collective-permute-start.17 = (bf16[512,768]{1,0:T(8,128)(2,1)S(1)}, bf16[512,768]{1,0:T(8,128)(2,1)S(1)}, u32[]{:S(2)}, u32[]{:S(2)}) collective-permute-start(bf16[512,768]{1,0:T(8,128)(2,1)S(1)} %pad_maximum_fusion.9), channel_id=1, source_target_pairs={{0,1},{1,0},{2,3},{3,2},{4,5},{5,4},{6,7},{7,6},{8,9},{9,8},{10,11... | collective-permute-start | bytes 2359304 | tf_op jit(solution)/shard_map/ppermute | solution.py:34
  324.7 38.0 %collective-permute-start.38 = (bf16[512,768]{1,0:T(8,128)(2,1)S(1)}, bf16[512,768]{1,0:T(8,128)(2,1)S(1)}, u32[]{:S(2)}, u32[]{:S(2)}) collective-permute-start(bf16[512,768]{1,0:T(8,128)(2,1)S(1)} %get-tuple-element.226), channel_id=1, source_target_pairs={{0,2},{1,3},{2,0},{3,1},{4,6},{5,7},{6,4},{7,5},{8,10},{9,11},{10,... | collective-permute-start | bytes 2359304 | tf_op jit(solution)/shard_map/ppermute | solution.py:34
  326.3 36.4 %collective-permute-start.40 = (bf16[512,768]{1,0:T(8,128)(2,1)S(1)}, bf16[512,768]{1,0:T(8,128)(2,1)S(1)}, u32[]{:S(2)}, u32[]{:S(2)}) collective-permute-start(bf16[512,768]{1,0:T(8,128)(2,1)S(1)} %get-tuple-element.227), channel_id=1, source_target_pairs={{0,1},{1,0},{2,3},{3,2},{4,5},{5,4},{6,7},{7,6},{8,9},{9,8},{10,11... | collective-permute-start | bytes 2359304 | tf_op jit(solution)/shard_map/ppermute | solution.py:34
  333.5 64.8 %collective-permute-start.42 = (bf16[512,768]{1,0:T(8,128)(2,1)}, bf16[512,768]{1,0:T(8,128)(2,1)S(1)}, u32[]{:S(2)}, u32[]{:S(2)}) collective-permute-start(bf16[512,768]{1,0:T(8,128)(2,1)} %get-tuple-element.230), channel_id=1, source_target_pairs={{0,2},{1,3},{2,0},{3,1},{4,6},{5,7},{6,4},{7,5},{8,10},{9,11},{10,... | collective-permute-start | bytes 2359304 | tf_op jit(solution)/shard_map/ppermute | solution.py:34
  335.0 63.3 %collective-permute-start.44 = (bf16[512,768]{1,0:T(8,128)(2,1)}, bf16[512,768]{1,0:T(8,128)(2,1)}, u32[]{:S(2)}, u32[]{:S(2)}) collective-permute-start(bf16[512,768]{1,0:T(8,128)(2,1)} %get-tuple-element.231), channel_id=1, source_target_pairs={{0,1},{1,0},{2,3},{3,2},{4,5},{5,4},{6,7},{7,6},{8,9},{9,8},{10,11... | collective-permute-start | bytes 2359304 | tf_op jit(solution)/shard_map/ppermute | solution.py:34
  365.9 38.2 %collective-permute-start.22 = (bf16[512,768]{0,1:T(8,128)(2,1)}, bf16[512,768]{0,1:T(8,128)(2,1)}, u32[]{:S(2)}, u32[]{:S(2)}) collective-permute-start(bf16[512,768]{0,1:T(8,128)(2,1)} %get-tuple-element.234), channel_id=1, source_target_pairs={{0,2},{1,3},{2,0},{3,1},{4,6},{5,7},{6,4},{7,5},{8,10},{9,11},{10,... | collective-permute-start | bytes 2359304 | tf_op jit(solution)/shard_map/ppermute | solution.py:34
  373.1 32.5 %collective-permute-start.24 = (bf16[512,768]{0,1:T(8,128)(2,1)}, bf16[512,768]{0,1:T(8,128)(2,1)}, u32[]{:S(2)}, u32[]{:S(2)}) collective-permute-start(bf16[512,768]{0,1:T(8,128)(2,1)} %get-tuple-element.235), channel_id=1, source_target_pairs={{0,1},{1,0},{2,3},{3,2},{4,5},{5,4},{6,7},{7,6},{8,9},{9,8},{10,11... | collective-permute-start | bytes 2359304 | tf_op jit(solution)/shard_map/ppermute | solution.py:34
  391.9 31.8 %collective-permute-start.34 = (bf16[512,768]{0,1:T(8,128)(2,1)}, bf16[512,768]{0,1:T(8,128)(2,1)S(1)}, u32[]{:S(2)}, u32[]{:S(2)}) collective-permute-start(bf16[512,768]{0,1:T(8,128)(2,1)} %get-tuple-element.238), channel_id=1, source_target_pairs={{0,2},{1,3},{2,0},{3,1},{4,6},{5,7},{6,4},{7,5},{8,10},{9,11},{10,... | collective-permute-start | bytes 2359304 | tf_op jit(solution)/shard_map/ppermute | solution.py:34
  408.4 29.5 %collective-permute-start.23 = (bf16[256,768]{0,1:T(8,128)(2,1)}, bf16[256,768]{0,1:T(8,128)(2,1)}, u32[]{:S(2)}, u32[]{:S(2)}) collective-permute-start(bf16[256,768]{0,1:T(8,128)(2,1)} %slice.380), channel_id=1, source_target_pairs={{0,1},{1,0},{2,3},{3,2},{4,5},{5,4},{6,7},{7,6},{8,9},{9,8},{10,11... | collective-permute-start | bytes 1179656 | tf_op jit(solution)/shard_map/ppermute | solution.py:34
  412.5 26.5 %collective-permute-start.25 = (bf16[256,768]{0,1:T(8,128)(2,1)}, bf16[256,768]{0,1:T(8,128)(2,1)}, u32[]{:S(2)}, u32[]{:S(2)}) collective-permute-start(bf16[256,768]{0,1:T(8,128)(2,1)} %slice.384), channel_id=1, source_target_pairs={{0,2},{1,3},{2,0},{3,1},{4,6},{5,7},{6,4},{7,5},{8,10},{9,11},{10,... | collective-permute-start | bytes 1179656 | tf_op jit(solution)/shard_map/ppermute | solution.py:34
  419.3 30.2 %all-to-all-start.7 = ((bf16[8,64,768]{2,1,0:T(8,128)(2,1)}), bf16[8,64,768]{2,1,0:T(8,128)(2,1)}, u32[]{:S(2)}, u32[]{:S(2)}) async-start(bf16[8,64,768]{2,1,0:T(8,128)(2,1)} %bitcast.76), calls=%async_computation.7 | async-start | bytes 1572864 | tf_op jit(solution)/shard_map/all_to_all | solution.py:131
  449.5 78.7 %all-to-all-start.2 = ((bf16[8,64,768]{2,1,0:T(8,128)(2,1)}), bf16[8,64,768]{2,1,0:T(8,128)(2,1)S(1)}, u32[]{:S(2)}, u32[]{:S(2)}) async-start(bf16[8,64,768]{2,1,0:T(8,128)(2,1)} %bitcast.63), calls=%async_computation.2 | async-start | bytes 1572864 | tf_op jit(solution)/shard_map/all_to_all | solution.py:131
  481.0 98.5 %collective-permute-start.53 = (bf16[4,96,896]{2,1,0:T(8,128)(2,1)}, bf16[4,96,896]{2,1,0:T(8,128)(2,1)}, u32[]{:S(2)}, u32[]{:S(2)}) collective-permute-start(bf16[4,96,896]{2,1,0:T(8,128)(2,1)} %fusion.77), channel_id=1, source_target_pairs={{0,4},{4,0},{8,12},{12,8},{16,20},{20,16},{24,28},{28,24},{1,5},{5... | collective-permute-start | bytes 2064392 | tf_op jit(solution)/shard_map/ppermute | solution.py:34
  528.1 45.9 %all-to-all-start.5 = ((bf16[8,64,768]{2,1,0:T(8,128)(2,1)}), bf16[8,64,768]{2,1,0:T(8,128)(2,1)S(1)}, u32[]{:S(2)}, u32[]{:S(2)}) async-start(bf16[8,64,768]{2,1,0:T(8,128)(2,1)} %bitcast.73), calls=%async_computation.5 | async-start | bytes 1572864 | tf_op jit(solution)/shard_map/all_to_all | solution.py:131
  573.5 36.3 %collective-permute-start.46 = (bf16[4,96,2432]{2,1,0:T(8,128)(2,1)}, bf16[4,96,2432]{2,1,0:T(8,128)(2,1)}, u32[]{:S(2)}, u32[]{:S(2)}) collective-permute-start(bf16[4,96,2432]{2,1,0:T(8,128)(2,1)} %fusion.35), channel_id=1, source_target_pairs={{0,4},{4,0},{8,12},{12,8},{16,20},{20,16},{24,28},{28,24},{1,5},{5... | collective-permute-start | bytes 5603336 | tf_op jit(solution)/shard_map/ppermute | solution.py:34
  (131 other events, 1682.0 us)

commit v2 on v1

v2 whole, which is shorter than its diff:
```python
import functools
import math

import jax
import jax.numpy as jnp
from jax import lax
from jax.experimental import pallas as pl
from jax.experimental.pallas import tpu as pltpu
from jax.sharding import PartitionSpec as P

HEADS = 12
HEAD_DIM = 64
FF = 3072


EPSILON = 1e-05
MOMENT = 0.9
KEEP_MEAN = 0.75
MASKED = -1e30
HEAD_ROWS = 16

BF16 = jnp.bfloat16
F32 = jnp.float32
NN = (((1,), (0,)), ((), ()))
NT = (((1,), (1,)), ((), ()))
TN = (((0,), (0,)), ((), ()))


def mm(left, right, dims=NN):
    return lax.dot_general(left, right, dims, preferred_element_type=F32)


def cost(micros):
    return pl.CostEstimate(flops=int(micros * 1e6), transcendentals=0, bytes_accessed=1 << 20)


def together(*values):
    return lax.optimization_barrier(values)


def after(value, *earlier):
    return lax.optimization_barrier((value, *earlier))[0]


def swap(values, axis_name, bits):
    size = lax.axis_size(axis_name)
    return lax.ppermute(values, axis_name, [(i, i ^ bits) for i in range(size)])


def bits_of(axis_name):
    return [1 << i for i in range(lax.axis_size(axis_name).bit_length() - 1)]


def device_number():
    return lax.axis_index("expert") * lax.axis_size("hidden") + lax.axis_index("hidden")


def to_experts(slots, dim=0):
    return lax.all_to_all(slots, "expert", split_axis=dim, concat_axis=dim, tiled=True)


def gather_far(block):
    far = [swap(block, "expert", 2 * k) for k in range(1, lax.axis_size("expert") // 2)]
    return jnp.stack([block, *far])


def gather_near(blocks, split):
    n_hidden = lax.axis_size("hidden")
    hidden_bits = bits_of("hidden")
    pieces = []
    for low, high, order in (
        (0, split, hidden_bits),
        (split, blocks.shape[2], hidden_bits[::-1]),
    ):
        part = blocks[:, :, low:high]
        places = [2 * k * n_hidden for k in range(part.shape[0])]
        for bit in order:
            part = jnp.concatenate([part, swap(part, "hidden", bit)], axis=0)
            places = places + [p ^ bit for p in places]
        pieces.append((part, places, low))
    return pieces


def gather_core(pieces):
    n_hidden = lax.axis_size("hidden")
    return pieces + [
        (swap(part, "expert", 1), [p ^ n_hidden for p in places], low)
        for part, places, low in pieces
    ]


def aligned(rows):
    return rows % 8 == 0


def as_operands(pieces):
    rows = pieces[0][0].shape[1]
    if aligned(rows):
        plan = [
            (index, row, place, low, part.shape[2])
            for index, (part, places, low) in enumerate(pieces)
            for row, place in enumerate(places)
        ]
        return [part for part, _, _ in pieces], plan
    columns = []
    for low in sorted({low for _, _, low in pieces}):
        some = [piece for piece in pieces if piece[2] == low]
        places = [p for _, places, _ in some for p in places]
        order = sorted(range(len(places)), key=lambda i: places[i])
        stacked = jnp.concatenate([part for part, _, _ in some], axis=0)[jnp.array(order)]
        columns.append(stacked)
    whole = jnp.concatenate(columns, axis=2)
    whole = whole[device_number() ^ jnp.arange(whole.shape[0])]
    return [whole.reshape(-1, whole.shape[2])], None


def place_pieces(plan, me, piece_refs, whole_ref, sems):
    if plan is None:
        return [pltpu.make_async_copy(piece_refs[0], whole_ref, sems.at[0])]
    rows = piece_refs[0].shape[1]
    copies = []
    for number, (index, row, place, low, width) in enumerate(plan):
        start = pl.multiple_of((me ^ place) * rows, 8)
        copies.append(
            pltpu.make_async_copy(
                piece_refs[index].at[row],
                whole_ref.at[pl.ds(start, rows), pl.ds(low, width)],
                sems.at[number],
            )
        )
    return copies


def sum_orders():
    n_hidden = lax.axis_size("hidden")
    n_far = lax.axis_size("expert") // 2
    hidden_bits = bits_of("hidden")
    orders = []
    for bits in (hidden_bits[::-1], hidden_bits):
        places = [2 * k * n_hidden for k in range(n_far)]
        for bit in bits[::-1]:
            places = places + [p ^ bit for p in places]
        orders.append(places + [p ^ n_hidden for p in places])
    return orders


def bundle(weight_in, weight_out):
    if weight_in.shape == weight_out.shape:
        return [jnp.stack([weight_in, weight_out])]
    return [weight_in[None], weight_out[None]]


def reduce_steps(kept, sent, split):
    hidden_bits = bits_of("hidden")
    n_far = lax.axis_size("expert") // 2
    (arrived,) = yield [swap(sent, "expert", 1)]
    total = kept + arrived.astype(F32)
    up, down = total[:, :split], total[:, split:]
    for up_bit, down_bit in zip(hidden_bits[::-1], hidden_bits):
        half = up.shape[0] // 2
        up_arrived, down_arrived = yield [
            swap(up[half:].astype(BF16), "hidden", up_bit),
            swap(down[half:].astype(BF16), "hidden", down_bit),
        ]
        up = up[:half] + up_arrived.astype(F32)
        down = down[:half] + down_arrived.astype(F32)
    total = jnp.concatenate([up, down], axis=1)
    rows = total.shape[0] // n_far
    away = total.astype(BF16)
    arrived = yield [
        swap(away[k * rows : (k + 1) * rows], "expert", 2 * k) for k in range(1, n_far)
    ]
    yield total[:rows] + sum(part.astype(F32) for part in arrived)


def behind(steps, arrived, *earlier):
    tied = together(*arrived, *earlier)
    return steps.send(tied[: len(arrived)]), tied[len(arrived) :]


def finish(steps, arrived):
    while isinstance(arrived, list):
        arrived = steps.send(arrived)
    return arrived


def spread(rows, bits):
    near = rows[None]
    for bit in bits[:-1]:
        near = jnp.concatenate([near, swap(near, "hidden", bit)], axis=0)
    return near, swap(near, "hidden", bits[-1])


def collect(near, far, bits):
    total = near + far.astype(F32)
    for bit in bits[-2::-1]:
        half = total.shape[0] // 2
        total = total[:half] + swap(total[half:].astype(BF16), "hidden", bit).astype(F32)
    return total.astype(BF16)


def head_parts(values, first_lane):
    lane = lax.broadcasted_iota(jnp.int32, values.shape, 1)
    return jnp.where(lane // HEAD_DIM == first_lane, values, 0.0)


def spare_lane(shape, head):
    lane = lax.broadcasted_iota(jnp.int32, shape, 1)
    return lane == (HEAD_DIM if head == 0 else 0)


def masked_keys(keys, head, length):
    key_pos = lax.broadcasted_iota(jnp.int32, keys.shape, 0)
    bias = jnp.where(key_pos < length, 0.0, MASKED)
    return jnp.where(spare_lane(keys.shape, head), bias, head_parts(keys, head)).astype(BF16)


def masked_queries(queries, head):
    return jnp.where(
        spare_lane(queries.shape, head), 1.0, head_parts(queries, head)
    ).astype(BF16)


def attend_forward_kernel(block, length_ref, q_ref, k_ref, v_ref, o_ref, rows_ref, lse_ref):
    pair = pl.program_id(0)
    length = length_ref[0]
    seq_len = q_ref.shape[0]
    scale = HEAD_DIM**-0.5
    queries = q_ref[...].astype(F32) * scale
    keys = k_ref[...].astype(F32)
    values = v_ref[...].astype(F32)

    @pl.when(pair == 0)
    def _():
        lse_ref[...] = jnp.zeros_like(lse_ref)

    heads = [
        (
            masked_queries(queries, head),
            masked_keys(keys, head, length),
            head_parts(values, head).astype(BF16),
        )
        for head in range(2)
    ]
    lane = lax.broadcasted_iota(jnp.int32, (block, 128), 1)
    on_diag = lax.broadcasted_iota(jnp.int32, (block, block), 0) >= lax.broadcasted_iota(
        jnp.int32, (block, block), 1
    )
    for index in range(seq_len // block):
        low, high = index * block, (index + 1) * block
        total = jnp.zeros((block, 128), F32)
        stats = lse_ref[low:high]
        for head in range(2):
            q_head, k_head, v_head = heads[head]
            diag = jnp.where(on_diag, mm(q_head[low:high], k_head[low:high], NT), MASKED)
            peak = jnp.max(diag, axis=1, keepdims=True)
            if index:
                past = mm(q_head[low:high], k_head[:low], NT)
                peak = jnp.maximum(peak, jnp.max(past, axis=1, keepdims=True))
            diag = jnp.exp(diag - peak)
            row_sum = jnp.sum(diag, axis=1, keepdims=True)
            mixed = mm(diag.astype(BF16), v_head[low:high])
            if index:
                past = jnp.exp(past - peak)
                row_sum = row_sum + jnp.sum(past, axis=1, keepdims=True)
                mixed = mixed + mm(past.astype(BF16), v_head[:low])
            total = total + mixed / row_sum
            stats = jnp.where(lane == 2 * pair + head, peak + jnp.log(row_sum), stats)
        o_ref[low:high] = total.astype(BF16)
        lse_ref[low:high] = stats

    @pl.when(pair == pl.num_programs(0) - 1)
    def _():
        rows_ref[...] = lse_ref[...].T[: rows_ref.shape[0]]


def attend_forward(qkv_rows, length, block):
    tok, width = qkv_rows.shape
    pairs = width // 3 // 128
    column = lambda offset: pl.BlockSpec((tok, 128), lambda i: (0, i + offset))
    return pl.pallas_call(
        functools.partial(attend_forward_kernel, block),
        grid=(pairs,),
        in_specs=[
            pl.BlockSpec(memory_space=pltpu.SMEM),
            column(0),
            column(pairs),
            column(2 * pairs),
        ],
        out_specs=[column(0), pl.BlockSpec((HEAD_ROWS, tok), lambda i: (0, 0))],
        out_shape=[
            jax.ShapeDtypeStruct((tok, pairs * 128), BF16),
            jax.ShapeDtypeStruct((HEAD_ROWS, tok), F32),
        ],
        scratch_shapes=[pltpu.VMEM((tok, 128), F32)],
        cost_estimate=cost(23),
        name="attend_forward",
    )(length, qkv_rows, qkv_rows, qkv_rows)


def attend_backward_kernel(
    block, first, length_ref, q_ref, k_ref, v_ref, g_ref, lse_ref, dot_ref, dq_ref, dk_ref, dv_ref,
    dk_acc, dv_acc
):
    length = length_ref[0]
    seq_len = q_ref.shape[0]
    scale = HEAD_DIM**-0.5
    queries = q_ref[...].astype(F32) * scale
    keys = k_ref[...].astype(F32)
    grads = g_ref[...].astype(F32)
    values = v_ref[...]
    heads = [
        (
            masked_queries(queries, head),
            masked_keys(keys, head, length),
            head_parts(queries, head).astype(BF16),
            head_parts(keys * scale, head).astype(BF16),
            head_parts(grads, head).astype(BF16),
        )
        for head in range(2)
    ]
    on_diag = lax.broadcasted_iota(jnp.int32, (block, block), 0) <= lax.broadcasted_iota(
        jnp.int32, (block, block), 1
    )
    dk_acc[...] = jnp.zeros_like(dk_acc)
    dv_acc[...] = jnp.zeros_like(dv_acc)
    for index in range(seq_len // block):
        low, high = index * block, (index + 1) * block
        grad_q = jnp.zeros((block, 128), F32)
        for head in range(2):
            q_aug, k_aug, q_head, k_head, g_head = heads[head]
            row = 2 * (first + pl.program_id(0)) + head
            lse = lse_ref[pl.ds(row, 1), low:high]
            row_dot = dot_ref[pl.ds(row, 1), low:high]
            for start, stop in ((0, low), (low, high)):
                if start == stop:
                    continue
                scores = mm(k_aug[start:stop], q_aug[low:high], NT)
                probs = jnp.exp(scores - lse)
                if start == low:
                    probs = jnp.where(on_diag, probs, 0.0)
                grad_p = mm(values[start:stop], g_head[low:high], NT)
                grad_s = (probs * (grad_p - row_dot)).astype(BF16)
                dv_acc[start:stop] += mm(probs.astype(BF16), g_head[low:high])
                dk_acc[start:stop] += mm(grad_s, q_head[low:high])
                grad_q = grad_q + mm(grad_s, k_head[start:stop], TN)
        dq_ref[low:high] = grad_q.astype(BF16)
    dk_ref[...] = dk_acc[...].astype(BF16)
    dv_ref[...] = dv_acc[...].astype(BF16)


def attend_backward(qkv_rows, grad_mixed, lse, row_dot, length, block, first, count):
    tok, width = qkv_rows.shape
    pairs = width // 3 // 128
    column = lambda offset: pl.BlockSpec((tok, 128), lambda i: (0, i + offset))
    whole = pl.BlockSpec((HEAD_ROWS, tok), lambda i: (0, 0))
    return pl.pallas_call(
        functools.partial(attend_backward_kernel, block, first),
        grid=(count,),
        in_specs=[
            pl.BlockSpec(memory_space=pltpu.SMEM),
            column(first),
            column(pairs + first),
            column(2 * pairs + first),
            column(first),
            whole,
            whole,
        ],
        out_specs=[column(0)] * 3,
        out_shape=[jax.ShapeDtypeStruct((tok, count * 128), BF16)] * 3,
        scratch_shapes=[pltpu.VMEM((tok, 128), F32)] * 2,
        cost_estimate=cost(17),
        name="attend_backward",
    )(length, qkv_rows, qkv_rows, qkv_rows, grad_mixed, lse, row_dot)


def centre(values):
    row_mean = jnp.mean(values, axis=-1, keepdims=True)
    centered = values - row_mean
    inverse = lax.rsqrt(jnp.mean(centered * centered, axis=-1, keepdims=True) + EPSILON)
    return centered * inverse, inverse


def norm_back(grad_rows, normed, inverse, gain_row):
    scaled = grad_rows * gain_row
    first_mean = jnp.mean(scaled, axis=-1, keepdims=True)
    second_mean = jnp.mean(scaled * normed, axis=-1, keepdims=True)
    return inverse * (scaled - first_mean - normed * second_mean)


def column_sums(ref, normed, grad_rows):
    @pl.when(pl.program_id(0) == 0)
    def _():
        ref[...] = jnp.zeros_like(ref)

    ref[0:1] += jnp.sum(grad_rows * normed, axis=0, keepdims=True)
    ref[1:2] += jnp.sum(grad_rows, axis=0, keepdims=True)


def any_space(count):
    return [pl.BlockSpec(memory_space=pl.ANY)] * count


def row_block(block, width):
    return pl.BlockSpec((block, width), lambda i: (i, 0))


def fixed(*shape):
    return pl.BlockSpec(shape, lambda i: (0,) * len(shape))


def project_in_kernel(plan, count, width, norm_low, me_ref, x_ref, *refs):
    piece_refs, (qkv_ref, attn_in_ref, whole_ref, norm_ref, sems) = refs[:count], refs[count:]
    copies = place_pieces(plan, me_ref[0], piece_refs, whole_ref, sems)
    first = pl.program_id(0) == 0

    @pl.when(first)
    def _():
        for copy in copies:
            copy.start()

    normed, _ = centre(x_ref[...].astype(F32))

    @pl.when(first)
    def _():
        for copy in copies:
            copy.wait()
        row = lax.broadcasted_iota(jnp.int32, (8, 128), 0)
        lane = lax.broadcasted_iota(jnp.int32, (8, 128), 1)
        norm_ref[...] = mm((row == lane).astype(BF16), whole_ref[:, norm_low : norm_low + 128], NT)

    attn_in = (normed * norm_ref[0:1] + norm_ref[1:2]).astype(BF16)
    attn_in_ref[...] = attn_in
    qkv_ref[...] = mm(attn_in, whole_ref[:, :width]).astype(BF16)


def project_in(inputs, pieces, width, norm_low, whole_width, block):
    tok, model_width = inputs.shape
    operands, plan = as_operands(pieces)
    return pl.pallas_call(
        functools.partial(project_in_kernel, plan, len(operands), width, norm_low),
        grid=(tok // block,),
        in_specs=[
            pl.BlockSpec(memory_space=pltpu.SMEM),
            row_block(block, model_width),
            *any_space(len(operands)),
        ],
        out_specs=[
            row_block(block, width),
            row_block(block, model_width),
            fixed(model_width, whole_width),
            fixed(8, model_width),
        ],
        out_shape=[
            jax.ShapeDtypeStruct((tok, width), BF16),
            jax.ShapeDtypeStruct((tok, model_width), BF16),
            jax.ShapeDtypeStruct((model_width, whole_width), BF16),
            jax.ShapeDtypeStruct((8, model_width), F32),
        ],
        scratch_shapes=[pltpu.SemaphoreType.DMA((len(plan) if plan else 1,))],
        cost_estimate=cost(9),
        name="project_in",
    )(device_number()[None], inputs, *operands)


def project_out_kernel(x_ref, o_ref, norm_ref, weight_ref, resid_ref, moe_in_ref):
    resid = x_ref[...].astype(F32) + mm(o_ref[...], weight_ref[...], NT)
    resid_ref[...] = resid
    normed, _ = centre(resid)
    moe_in_ref[...] = (normed * norm_ref[2:3] + norm_ref[3:4]).astype(BF16)


def columns_of(array, low, width):
    assert low % width == 0
    return pl.BlockSpec((array.shape[0], width), lambda i: (0, low // width))


def project_out(inputs, attn_out, norm_rows, weight, low, block):
    tok, width = inputs.shape
    return pl.pallas_call(
        project_out_kernel,
        grid=(tok // block,),
        in_specs=[
            row_block(block, width),
            row_block(block, width),
            fixed(8, width),
            columns_of(weight, low, width),
        ],
        out_specs=[row_block(block, width), row_block(block, width)],
        out_shape=[
            jax.ShapeDtypeStruct((tok, width), F32),
            jax.ShapeDtypeStruct((tok, width), BF16),
        ],
        cost_estimate=cost(7),
        name="project_out",
    )(inputs, attn_out, norm_rows, weight)


def middle_back_kernel(
    select_ref, first_ref, second_ref, resid_ref, grad_ref, o_ref, norm_ref, weight_ref,
    grad_mid_ref, branch_ref, grad_attn_ref, dot_ref, sums_ref
):
    width = resid_ref.shape[1]
    count = first_ref.shape[0]
    grad_rows = mm(select_ref[:, :count], first_ref[...])
    grad_rows = grad_rows + mm(select_ref[:, count:], second_ref[...])
    normed, inverse = centre(resid_ref[...])
    grad_mid = grad_ref[...].astype(F32) + norm_back(grad_rows, normed, inverse, norm_ref[2:3])
    column_sums(sums_ref, normed, grad_rows)
    grad_mid_ref[...] = grad_mid
    branch = grad_mid.astype(BF16)
    branch_ref[...] = branch
    grad_attn = mm(branch, weight_ref[...]).astype(BF16)
    grad_attn_ref[...] = grad_attn
    product = grad_attn.astype(F32) * o_ref[...].astype(F32)
    upper = product.astype(BF16)
    lower = (product - upper.astype(F32)).astype(BF16)
    head = lax.broadcasted_iota(jnp.int32, (HEAD_ROWS, width), 0)
    lane = lax.broadcasted_iota(jnp.int32, (HEAD_ROWS, width), 1)
    ones = (lane // HEAD_DIM == head).astype(BF16)
    dot_ref[...] = mm(ones, upper, NT) + mm(ones, lower, NT)


def middle_back(select, first, second, resid, grad_out, attn_out, norm_rows, weight, low, block):
    tok, width = resid.shape
    return pl.pallas_call(
        middle_back_kernel,
        grid=(tok // block,),
        in_specs=[
            row_block(block, select.shape[1]),
            fixed(*first.shape),
            fixed(*second.shape),
            row_block(block, width),
            row_block(block, width),
            row_block(block, width),
            fixed(8, width),
            columns_of(weight, low, width),
        ],
        out_specs=[
            row_block(block, width),
            row_block(block, width),
            row_block(block, width),
            pl.BlockSpec((HEAD_ROWS, block), lambda i: (0, i)),
            fixed(8, width),
        ],
        out_shape=[
            jax.ShapeDtypeStruct((tok, width), F32),
            jax.ShapeDtypeStruct((tok, width), BF16),
            jax.ShapeDtypeStruct((tok, width), BF16),
            jax.ShapeDtypeStruct((HEAD_ROWS, tok), F32),
            jax.ShapeDtypeStruct((8, width), F32),
        ],
        cost_estimate=cost(12),
        name="middle_back",
    )(select, first, second, resid, grad_out, attn_out, norm_rows, weight)


def last_back_kernel(
    spans, count, x_ref, grad_mid_ref, norm_ref, weight_ref, *refs
):
    grad_refs, (out_ref, sums_ref) = refs[:count], refs[count:]
    grad_rows = None
    for ref, low in zip(grad_refs, spans):
        term = mm(ref[...], weight_ref[:, low : low + ref.shape[1]], NT)
        grad_rows = term if grad_rows is None else grad_rows + term
    normed, inverse = centre(x_ref[...].astype(F32))
    out_ref[...] = grad_mid_ref[...] + norm_back(grad_rows, normed, inverse, norm_ref[0:1])
    column_sums(sums_ref, normed, grad_rows)


def last_back(inputs, grad_mid, norm_rows, weight, grads, spans, block):
    tok, width = inputs.shape
    return pl.pallas_call(
        functools.partial(last_back_kernel, spans, len(grads)),
        grid=(tok // block,),
        in_specs=[
            row_block(block, width),
            row_block(block, width),
            fixed(8, width),
            columns_of(weight, 0, 3 * width),
            *[row_block(block, grad.shape[1]) for grad in grads],
        ],
        out_specs=[row_block(block, width), fixed(8, width)],
        out_shape=[
            jax.ShapeDtypeStruct((tok, width), F32),
            jax.ShapeDtypeStruct((8, width), F32),
        ],
        cost_estimate=cost(11),
        name="last_back",
    )(inputs, grad_mid, norm_rows, weight, *grads)


def fill_sums(total_ref, pairs, extra_refs, row_refs):
    low = 0
    for left_ref, right_ref in pairs:
        high = low + right_ref.shape[1]
        total_ref[:, low:high] = mm(left_ref[...], right_ref[...], TN)
        low = high
    for ref in extra_refs:
        total_ref[:, low : low + ref.shape[1]] = ref[...]
        low += ref.shape[1]
    if row_refs:
        rows = [ref[...] for ref in row_refs]
        pad = 128 - sum(part.shape[0] for part in rows)
        rows.append(jnp.zeros((pad, rows[0].shape[1]), F32))
        total_ref[:, low : low + 128] = jnp.concatenate(rows, axis=0).T


def weight_sums_kernel(orders, rows, split, index, me_ref, *refs):
    lefts, rights, extras, row_parts, refs = (
        refs[: index[0]], refs[index[0] : index[1]], refs[index[1] : index[2]],
        refs[index[2] : index[3]], refs[index[3] :],
    )
    pairs = [(lefts[min(k, len(lefts) - 1)], right) for k, right in enumerate(rights)]
    if orders is None:
        fill_sums(refs[0], pairs, extras, row_parts)
        return
    keep, send, total_ref = refs
    fill_sums(total_ref, pairs, extras, row_parts)
    me = me_ref[0]
    for order, first, last in ((orders[0], 0, split), (orders[1], split, keep.shape[1])):
        half = len(order) // 2
        for place, relative in enumerate(order):
            start = pl.multiple_of((me ^ relative) * rows, 8)
            value = total_ref[pl.ds(start, rows), first:last]
            if place < half:
                keep[place * rows : (place + 1) * rows, first:last] = value
            else:
                low = (place - half) * rows
                send[low : low + rows, first:last] = value.astype(BF16)


def weight_sums(lefts, rights, extras, row_parts, split, rows):
    width = sum(array.shape[1] for array in (*rights, *extras)) + (128 if row_parts else 0)
    model_width = lefts[0].shape[1]
    orders = sum_orders()
    half = model_width // 2
    arrays = (*lefts, *rights, *extras, *row_parts)
    index = [len(lefts), len(lefts) + len(rights)]
    index += [index[1] + len(extras), len(arrays)]
    direct = aligned(rows)
    call = pl.pallas_call(
        functools.partial(weight_sums_kernel, orders if direct else None, rows, split, index),
        grid=(1,),
        in_specs=[
            pl.BlockSpec(memory_space=pltpu.SMEM),
            *[fixed(*array.shape) for array in arrays],
        ],
        out_specs=[fixed(half, width)] * 2 if direct else [fixed(model_width, width)],
        out_shape=(
            [jax.ShapeDtypeStruct((half, width), dtype) for dtype in (F32, BF16)]
            if direct
            else [jax.ShapeDtypeStruct((model_width, width), F32)]
        ),
        scratch_shapes=[pltpu.VMEM((model_width, width), F32)] if direct else [],
        cost_estimate=cost(6),
        name="weight_sums",
    )(device_number()[None], *arrays)
    if direct:
        return call
    blocks = call[0].reshape(-1, rows, width)
    ordered = [
        blocks[device_number() ^ jnp.array(order)].reshape(model_width, width)[:, columns]
        for order, columns in zip(orders, (slice(0, split), slice(split, width)))
    ]
    total = jnp.concatenate(ordered, axis=1)
    return total[:half], total[half:].astype(BF16)


def expert_kernel(
    me_ref, rows_ref, group_ref, router_ref, in_own, out_own, in_far, out_far,
    act_ref, grad_pre_ref, pair_ref, gate_ref, logit_ref, grad_ref,
    back_sum, total_ref
):
    step, steps = pl.program_id(0), pl.num_programs(0)
    width = rows_ref.shape[1]
    lane = lax.broadcasted_iota(jnp.int32, (rows_ref.shape[0], 128), 1)

    @pl.when(step == 0)
    def _():
        own = me_ref[0]
        route = group_ref[0, :, width:].astype(F32)
        other = (route[:, 0:1] + route[:, 1:2]).astype(jnp.int32) - own
        signs = (lane == own).astype(F32) - (lane == other).astype(F32)
        gap = jnp.sum(mm(rows_ref[...], router_ref[...]) * signs, axis=1, keepdims=True)
        gate = jax.nn.sigmoid(gap)
        gate_ref[...] = jnp.broadcast_to(gate, gate_ref.shape)
        logit_ref[...] = signs.astype(BF16)
        pair_ref[...] = (gate * group_ref[0, :, :width].astype(F32)).astype(BF16)
        back_sum[...] = jnp.zeros_like(back_sum)
        total_ref[...] = jnp.zeros_like(total_ref)

    def chunk(weight_in, weight_out):
        back = mm(group_ref[0, :, :width], weight_out, NT)
        pre_act = mm(rows_ref[...], weight_in)
        gate = gate_ref[:, 0:1]
        root = math.sqrt(2.0 / math.pi)
        squared = pre_act * pre_act
        curve = jnp.tanh(pre_act * (root + (root * 0.044715) * squared))
        half = 0.5 * (1.0 + curve)
        activation = (pre_act * half).astype(BF16)
        slope = half + pre_act * (half * (1.0 - curve)) * (root + (3 * root * 0.044715) * squared)
        grad_pre = (slope * (gate * back)).astype(BF16)
        act_ref[0] = activation
        grad_pre_ref[0] = grad_pre
        product = activation.astype(F32) * back
        partial = product[:, :128]
        for low in range(128, product.shape[1], 128):
            partial = partial + product[:, low : low + 128]
        back_sum[...] += partial
        total_ref[...] += mm(grad_pre, weight_in, NT)

    @pl.when(step < steps // 2)
    def _():
        chunk(in_own[0], out_own[0])

    @pl.when(step >= steps // 2)
    def _():
        chunk(in_far[0], out_far[0])

    @pl.when(step == steps - 1)
    def _():
        gate = gate_ref[:, 0:1]
        grad_gate = jnp.sum(back_sum[...], axis=1, keepdims=True)
        signs = logit_ref[...].astype(F32)
        grad_logit = (gate * (1.0 - gate) * grad_gate * signs).astype(BF16)
        logit_ref[...] = grad_logit
        grad_ref[...] = (total_ref[...] + mm(grad_logit, router_ref[...], NT)).astype(grad_ref.dtype)


def expert_pass(own, part, rows, groups, weight, low, local, other, dtype):
    count, width = rows.shape
    units = local[0].shape[2]
    last = 1 if len(local) == 1 else 0
    parts = 2 if units % 256 == 0 else 1
    wide = units // parts
    near = lambda c: jnp.minimum(c, parts - 1)
    far = lambda c: jnp.maximum(c - parts, 0)
    hidden = pl.BlockSpec((1, count, wide), lambda c: (c // parts, 0, c % parts))
    return pl.pallas_call(
        expert_kernel,
        grid=(2 * parts,),
        in_specs=[
            pl.BlockSpec(memory_space=pltpu.SMEM),
            fixed(count, width),
            pl.BlockSpec((1, count, width + 128), lambda c: (part, 0, 0)),
            columns_of(weight, low, 128),
            pl.BlockSpec((1, width, wide), lambda c: (0, 0, near(c))),
            pl.BlockSpec((1, wide, width), lambda c: (last, near(c), 0)),
            pl.BlockSpec((1, width, wide), lambda c: (0, 0, far(c))),
            pl.BlockSpec((1, wide, width), lambda c: (last, far(c), 0)),
        ],
        out_specs=[
            hidden,
            hidden,
            fixed(count, width),
            fixed(count, 128),
            fixed(count, 128),
            fixed(count, width),
        ],
        out_shape=[
            jax.ShapeDtypeStruct((2, count, units), BF16),
            jax.ShapeDtypeStruct((2, count, units), BF16),
            jax.ShapeDtypeStruct((count, width), BF16),
            jax.ShapeDtypeStruct((count, 128), F32),
            jax.ShapeDtypeStruct((count, 128), BF16),
            jax.ShapeDtypeStruct((count, width), dtype),
        ],
        scratch_shapes=[pltpu.VMEM((count, 128), F32), pltpu.VMEM((count, width), F32)],
        cost_estimate=cost(10),
        name="expert_pass",
    )(own[None], rows, groups, weight, local[0], local[-1], other[0], other[-1])


def nesterov(master, momentum, average, grad_full, rate):
    moment_new = MOMENT * momentum + grad_full
    weight_new = master - rate * (grad_full + MOMENT * moment_new)
    return (grad_full, moment_new, weight_new, KEEP_MEAN * average + (1.0 - KEEP_MEAN) * weight_new)


def per_device(
    inputs,
    out_grad,
    seq_lengths,
    routes,
    norm_master,
    norm_momentum,
    norm_average,
    qkv_master,
    qkv_momentum,
    qkv_average,
    proj_master,
    proj_momentum,
    proj_average,
    router_master,
    router_momentum,
    router_average,
    frozen_in,
    frozen_out,
    expert_in_master,
    expert_in_momentum,
    expert_in_average,
    expert_out_master,
    expert_out_momentum,
    expert_out_average,
):
    tok_dev, model_width = inputs.shape
    seq_dev = seq_lengths.shape[0]
    assert seq_dev == 1
    n_expert = lax.axis_size("expert")
    n_hidden = lax.axis_size("hidden")
    experts = 2 * n_expert
    capacity = tok_dev * 2 // experts // 2
    slot_count = experts * capacity
    tokens_all = tok_dev * n_expert * n_hidden
    own_rows = model_width // (n_expert * n_hidden)
    block_rows = min(256, tok_dev)
    qkv_width = 3 * model_width
    expert_index = lax.axis_index("expert")
    hidden_bits = bits_of("hidden")
    weight_bit, token_bits = hidden_bits[0], hidden_bits[1:]

    proj_low, router_low = qkv_width, qkv_width + model_width
    norm_low, whole_width = router_low + 128, router_low + 256
    own_block = jnp.concatenate(
        [
            qkv_master,
            proj_master.T,
            router_master,
            jnp.zeros((own_rows, 128 - experts), F32),
            norm_master.T,
            jnp.zeros((own_rows, 124), F32),
        ],
        axis=1,
    ).astype(BF16)
    far_blocks = gather_far(own_block)

    row_ids = jnp.arange(tok_dev, dtype=jnp.int32)
    live_rows = row_ids < seq_lengths[0]
    live_float = live_rows.astype(F32)[:, None]
    expert_ids = jnp.arange(128, dtype=jnp.int32)
    match = [routes[:, k : k + 1] == expert_ids[None, :] for k in range(2)]
    counts = ((match[0] | match[1]) & live_rows[:, None]).astype(BF16)
    earlier = (row_ids[:, None] > row_ids[None, :]).astype(BF16)
    before = mm(earlier, counts)
    slot_ids = jnp.arange(slot_count, dtype=jnp.int32)
    chosen = None
    for k in range(2):
        rank = jnp.sum(jnp.where(match[k], before, 0.0), axis=1).astype(jnp.int32)
        kept = live_rows & (rank < capacity)
        expert_of = routes[:, k]
        slot = (expert_of % 2 * n_expert + expert_of // 2) * capacity + rank
        hit = jnp.where(kept, slot, -1)[:, None] == slot_ids[None, :]
        chosen = hit if chosen is None else chosen | hit
    select = chosen.astype(BF16)
    route_part = jnp.concatenate(
        [routes.astype(BF16), jnp.zeros((tok_dev, 126), BF16)], axis=1
    )
    grad_out_rows = jnp.where(live_rows[:, None], out_grad, jnp.zeros_like(out_grad))
    early = jnp.concatenate([grad_out_rows, route_part], axis=1)
    early_slots = mm(select, early, TN).astype(BF16)

    far_blocks, early_slots = together(far_blocks, early_slots)
    early_arrived = to_experts(
        early_slots.reshape(2, n_expert, capacity, model_width + 128), 1
    )
    pieces = gather_near(far_blocks, whole_width // 2 // 128 * 128)
    local_weights = [
        bundle(frozen_in[0], frozen_out[0]),
        bundle(expert_in_master[0].astype(BF16), expert_out_master[0].astype(BF16)),
    ]
    parts, sent = together([part for part, _, _ in pieces], local_weights)
    other_weights = [[swap(part, "hidden", weight_bit) for part in some] for some in sent]
    pieces = gather_core([(part, *rest) for part, (_, *rest) in zip(parts, pieces)])

    qkv_rows, attn_in, weights, norm_rows = project_in(
        inputs, pieces, qkv_width, norm_low, whole_width, block_rows
    )
    qkv_rows, early_arrived = together(qkv_rows, early_arrived)
    early_near, early_far = spread(early_arrived.reshape(-1, model_width + 128), token_bits)
    attn_out, log_rows = attend_forward(qkv_rows, seq_lengths, block_rows)
    attn_out, other_weights[0] = together(attn_out, other_weights[0])
    resid_mid, moe_in = project_out(
        inputs, attn_out, norm_rows, weights, proj_low, block_rows
    )

    moe_slots = mm(select, moe_in, TN).astype(BF16)
    moe_slots, early_far = together(moe_slots, early_far)
    moe_slots = moe_slots.reshape(2, n_expert, capacity, model_width)
    spread_rows = n_hidden // 4 if n_hidden > 2 else 1
    group_rows = n_expert * capacity
    early_near, early_far = [
        early.reshape(spread_rows, 2, group_rows, model_width + 128)
        .swapaxes(0, 1)
        .reshape(2, spread_rows * group_rows, model_width + 128)
        for early in (early_near, early_far)
    ]

    def expert(part, rows, groups, dtype):
        *kept, grad = expert_pass(
            2 * expert_index + part,
            part,
            rows.reshape(-1, model_width),
            groups,
            weights,
            router_low,
            local_weights[part],
            other_weights[part],
            dtype,
        )
        return (rows.reshape(-1, model_width), *kept), grad.reshape(rows.shape)

    def home(near, far):
        total = collect(near, far, token_bits)
        return to_experts(total.reshape(n_expert, capacity, model_width)).reshape(-1, model_width)

    near_rows, far_rows = spread(to_experts(moe_slots[0]).reshape(-1, model_width), token_bits)
    near_first, near_grad = expert(0, near_rows, early_near, F32)
    arrived = to_experts(moe_slots[1]).reshape(-1, model_width)
    far_rows, arrived, near_grad = together(far_rows, arrived, near_grad)
    near_rows, next_rows = spread(arrived, token_bits)
    far_first, far_grad = expert(0, far_rows, early_far, BF16)
    near_rows, far_grad = together(near_rows, far_grad)
    far_arrived = swap(far_grad, "hidden", token_bits[-1])
    near_second, next_grad = expert(1, near_rows, early_near, F32)
    next_rows, next_grad = together(next_rows, next_grad)
    far_second, last_grad = expert(1, next_rows, early_far, BF16)
    far_arrived, last_grad = together(far_arrived, last_grad)
    back_first = home(near_grad, far_arrived)
    last_arrived = swap(last_grad, "hidden", token_bits[-1])

    terms = None
    for rows, activation, grad_pre, pair_grad, _, grad_logit in (near_second, far_second):
        activation, grad_pre, grad_logit, last_grad = together(
            activation, grad_pre, grad_logit, last_grad
        )
        new = [mm(rows, grad_pre[k], TN) for k in range(2)]
        new += [mm(activation[k], pair_grad, TN) for k in range(2)]
        terms = new if terms is None else [a + b for a, b in zip(terms, new)]
    away = bundle(terms[1].astype(BF16), terms[3].astype(BF16))
    last_arrived, away = together(last_arrived, away)
    back_second = home(next_grad, last_arrived)
    away = [swap(part, "hidden", weight_bit) for part in away]

    values, router_part = [], 0.0
    for part, (near, far) in enumerate(((near_first, far_first), (near_second, far_second))):
        pair = []
        for rows, activation, grad_pre, pair_grad, gate, grad_logit in (near, far):
            activation, grad_logit, last_arrived = together(activation, grad_logit, last_arrived)
            value = mm(activation[0], local_weights[part][-1][-1])
            value = value + mm(activation[1], other_weights[part][-1][-1])
            pair.append((gate[:, 0:1] * value).reshape(-1, group_rows, model_width))
            router_part = router_part + mm(rows, grad_logit, TN)
        values.append((pair[0], swap(pair[1].astype(BF16), "hidden", token_bits[-1])))
    back_first, back_second, router_part = together(back_first, back_second, router_part)

    grad_mid, grad_branch, grad_attn, row_dot, sums_two = middle_back(
        select, back_first, back_second, resid_mid, grad_out_rows, attn_out, norm_rows, weights,
        proj_low, block_rows
    )
    pairs = HEADS // 2

    def backward(first, count):
        return attend_backward(
            qkv_rows, grad_attn, log_rows, row_dot, seq_lengths, block_rows, first, count
        )

    grads_a = backward(0, pairs // 2)
    far_a, far_b, *grads_a = together(values[0][1], values[1][1], *grads_a)
    values_a = home(values[0][0], far_a)
    split_a = 1024
    sums_a = weight_sums(
        (grad_branch, attn_in), (attn_out, *grads_a), (router_part,), (), split_a, own_rows
    )
    grad_attn, *sums_a = together(grad_attn, *sums_a)
    steps_a = reduce_steps(*sums_a, split_a)
    there_a = next(steps_a)
    grads_b = backward(pairs // 2, pairs // 2 - 1)
    there_a, (grad_attn, values_a, *grads_b) = behind(
        steps_a, there_a, grad_attn, values_a, *grads_b
    )
    values_b = home(values[1][0], far_b)
    grads_c = backward(pairs - 1, 1)
    there_a, grads_c = behind(steps_a, there_a, *grads_c)
    grad_parts = [*grads_a, *grads_b, *grads_c]
    spans = [128 * (first + pairs * k) for first in (0, pairs // 2, pairs - 1) for k in range(3)]
    input_grad, sums_one = last_back(
        inputs, grad_mid, norm_rows, weights, grad_parts, spans, block_rows
    )
    there_a, (sums_one,) = behind(steps_a, there_a, sums_one)
    split_b = 640
    sums_b = weight_sums(
        (attn_in,),
        [part for pair in zip(grads_b, grads_c) for part in pair],
        (),
        (sums_one, sums_two),
        split_b,
        own_rows,
    )
    there_a, sums_b = behind(steps_a, there_a, *sums_b)
    done_a = finish(steps_a, there_a)
    steps_b = reduce_steps(*sums_b, split_b)
    there_b = next(steps_b)
    in_grad = terms[0] + away[0][0].astype(F32)
    out_grad_sum = terms[2] + away[-1][-1].astype(F32)
    done_b = finish(steps_b, there_b)
    outputs = (
        live_float
        * (
            resid_mid
            + mm(select[:, : slot_count // 2], values_a)
            + mm(select[:, slot_count // 2 :], values_b)
        )
    ).astype(BF16)

    proj_sum = done_a[:, :model_width].T
    first_qkv = done_a[:, model_width : model_width + qkv_width // 2]
    router_sum = done_a[:, model_width + qkv_width // 2 :][:, :experts]
    second_qkv = done_b[:, : qkv_width // 2]
    qkv_sum = jnp.concatenate(
        [first_qkv.reshape(own_rows, 3, -1), second_qkv.reshape(own_rows, 3, -1)], axis=2
    ).reshape(own_rows, qkv_width)
    norm_columns = done_b[:, qkv_width // 2 :]
    norm_sum = jnp.concatenate([norm_columns[:, 0:2], norm_columns[:, 8:10]], axis=1).T

    norm_rate = 0.1 / math.sqrt(tokens_all)
    qkv_rate = 1.0 / math.sqrt(model_width * tokens_all)
    proj_rate = 40.0 / math.sqrt(model_width * tokens_all)
    router_rate = 0.08 * math.sqrt(experts / (model_width * tokens_all))
    in_rate = 5.0 * math.sqrt(experts / (model_width * tokens_all))
    out_rate = 2.5 * math.sqrt(experts / (FF * tokens_all))
    norm_set = nesterov(norm_master, norm_momentum, norm_average, norm_sum, norm_rate)
    qkv_set = nesterov(qkv_master, qkv_momentum, qkv_average, qkv_sum, qkv_rate)
    proj_set = nesterov(proj_master, proj_momentum, proj_average, proj_sum, proj_rate)
    router_set = nesterov(router_master, router_momentum, router_average, router_sum, router_rate)
    in_set = nesterov(
        expert_in_master, expert_in_momentum, expert_in_average, in_grad[None], in_rate
    )
    out_set = nesterov(
        expert_out_master, expert_out_momentum, expert_out_average, out_grad_sum[None], out_rate
    )
    return (
        outputs,
        input_grad,
        *norm_set,
        *qkv_set,
        *proj_set,
        *router_set,
        *in_set,
        *out_set,
    )


def solution(mesh):
    rows = P(("expert", "hidden"), None)
    columns = P(None, ("expert", "hidden"))
    expert_in = P("expert", None, "hidden")
    expert_out = P("expert", "hidden", None)
    return jax.shard_map(
        per_device,
        mesh=mesh,
        in_specs=(
            rows,
            rows,
            P(("expert", "hidden")),
            rows,
            *[columns] * 3,
            *[rows] * 3,
            *[columns] * 3,
            *[rows] * 3,
            expert_in,
            expert_out,
            *[expert_in] * 3,
            *[expert_out] * 3,
        ),
        out_specs=(
            rows,
            rows,
            *[columns] * 4,
            *[rows] * 4,
            *[columns] * 4,
            *[rows] * 4,
            *[expert_in] * 4,
            *[expert_out] * 4,
        ),
        check_vma=False,
    )
```

time: 678 us -> 492 us (0.73)
  Pallas kernels: 55.2 us -> 168 us
  local copies, waits for them, and re-layouts: 138 us -> 29.3 us
  matrix products: 122 us -> 64.4 us
  other arithmetic: 80.7 us -> 32.7 us
  waiting for transfers between devices: 164 us -> 117 us
  starting transfers between devices: 105 us -> 71.8 us
    pallas_call x1 -> x13, Pallas kernels: 31.9 us -> 146 us  [the longest x4 52.1 us: expert_pass(): pl.pallas_call(expert_kernel, grid=(2 * parts,), in_specs=[pl.BlockSpec(m...]
    ppermute x60 -> x35, waiting for transfers between devices: 158 us -> 77.6 us  [swap(): return lax.ppermute(values, axis_name, [(i, i ^ bits) for i in range(size)])]
    dot_general x27 -> x25, matrix products: 119 us -> 64.4 us  [mm(): return lax.dot_general(left, right, dims, preferred_element_type=F32)]
    unnamed x230 -> x147, local copies, waits for them, and re-layouts: 57.8 us -> 15 us
    all_to_all x8 -> x7, waiting for transfers between devices: 6.62 us -> 39.4 us  [to_experts(): lax.all_to_all(slots, 'expert', split_axis=dim, concat_axis=dim, tiled=True)]
    concatenate x22 -> x2, local copies, waits for them, and re-layouts: 33 us -> 0.84 us  [per_device(): jnp.concatenate([qkv_master, proj_master.T, router_master, jnp.zeros((own...]
    ppermute x60 -> x35, starting transfers between devices: 67.5 us -> 42.5 us  [swap(): return lax.ppermute(values, axis_name, [(i, i ^ bits) for i in range(size)])]
    slice x28 -> x19, local copies, waits for them, and re-layouts: 23.5 us -> 6.81 us  [the longest x4 3.64 us: per_device(): pair.append((gate[:, 0:1] * value).reshape(-1, group_rows, model_width))]
  transfers between devices with their start and end apart: 68 -> 42, of which waited for: 35 -> 18; matrix products, arithmetic and copies ran while one was open for 42% -> 22% of each run, Pallas kernels for 8% -> 33%
where the time goes in v2:
time: 492 us; the launch traced here: 486 us
  Pallas kernels  168 us (34%)
  waiting for transfers between devices  117 us (24%)
  starting transfers between devices  71.8 us (15%)
  matrix products  64.4 us (13%)
  other arithmetic  32.7 us (7%)
  local copies, waits for them, and re-layouts  29.3 us (6%)
    ppermute x35, waiting for transfers between devices, swap(): return lax.ppermute(values, axis_name, [(i, i ^ bits) for i in range(size)])  77.6 us
    dot_general x25, matrix products, mm(): return lax.dot_general(left, right, dims, preferred_element_type=F32)  64.4 us
    pallas_call x4, Pallas kernels, expert_pass(): pl.pallas_call(expert_kernel, grid=(2 * parts,), in_specs=[pl.BlockSpec(m...  52.1 us
    ppermute x35, starting transfers between devices, swap(): return lax.ppermute(values, axis_name, [(i, i ^ bits) for i in range(size)])  42.5 us
    all_to_all x7, waiting for transfers between devices, to_experts(): lax.all_to_all(slots, 'expert', split_axis=dim, concat_axis=dim, tiled=True)  39.4 us
    pallas_call x3, Pallas kernels, attend_backward(): pl.pallas_call(functools.partial(attend_backward_kernel, block, first), g...  36.5 us
    all_to_all x7, starting transfers between devices, to_experts(): lax.all_to_all(slots, 'expert', split_axis=dim, concat_axis=dim, tiled=True)  29.3 us
    pallas_call x1, Pallas kernels, attend_forward(): pl.pallas_call(functools.partial(attend_forward_kernel, block), grid=(pai...  22.7 us
  transfers between devices with their start and end apart: 42, of which 18 were waited for; matrix products, arithmetic and copies ran while one was open for 22% of the time, Pallas kernels for 33%

profile of v2, /device:TPU:0, one launch (start us, length us, event | category | flops | bytes accessed | tf_op | source)
XLA Modules:
  0.0 486.2 jit_solution(15574012692318459339)
XLA Ops:
  4.9 5.0 %collective-permute-start.2 = (bf16[24,3328]{1,0:T(8,128)(2,1)}, bf16[24,3328]{1,0:T(8,128)(2,1)S(1)}, u32[]{:S(2)}, u32[]{:S(2)}) collective-permute-start(bf16[24,3328]{1,0:T(8,128)(2,1)} %concatenate.56), channel_id=1, source_target_pairs={{0,24},{4,28},{8,16},{12,20},{16,8},{20,12},{24,0},{28,4},{1,25},{... | collective-permute-start | bytes 479240 | tf_op jit(solution)/shard_map/ppermute | solution.py:47
  18.6 5.0 %collective-permute-done.1 = bf16[24,3328]{1,0:T(8,128)(2,1)S(1)} collective-permute-done((bf16[24,3328]{1,0:T(8,128)(2,1)}, bf16[24,3328]{1,0:T(8,128)(2,1)S(1)}, u32[]{:S(2)}, u32[]{:S(2)}) %collective-permute-start.1) | collective-permute-done | bytes 159776 | tf_op jit(solution)/shard_map/ppermute | solution.py:47
  25.1 4.5 all-to-all-start
  32.8 6.9 %collective-permute-done.5 = bf16[4,24,1664]{2,1,0:T(8,128)(2,1)S(1)} collective-permute-done((bf16[4,24,1664]{2,1,0:T(8,128)(2,1)S(1)}, bf16[4,24,1664]{2,1,0:T(8,128)(2,1)S(1)}, u32[]{:S(2)}, u32[]{:S(2)}) %collective-permute-start.5) | collective-permute-done | bytes 319520 | tf_op jit(solution)/shard_map/ppermute | solution.py:47
  48.7 7.1 %collective-permute-done.6 = bf16[8,24,1664]{2,1,0:T(8,128)(2,1)S(1)} collective-permute-done((bf16[8,24,1664]{2,1,0:T(8,128)(2,1)S(1)}, bf16[8,24,1664]{2,1,0:T(8,128)(2,1)S(1)}, u32[]{:S(2)}, u32[]{:S(2)}) %collective-permute-start.6) | collective-permute-done | bytes 639008 | tf_op jit(solution)/shard_map/ppermute | solution.py:47
  63.6 11.4 %project_in.1 = (bf16[1024,2304]{1,0:T(8,128)(2,1)}, bf16[1024,768]{1,0:T(8,128)(2,1)}, bf16[768,3328]{1,0:T(8,128)(2,1)}, f32[8,768]{1,0:T(8,128)}) custom-call(s32[1]{0:T(128)} %bitcast.1.me_ref, bf16[1024,768]{1,0:T(8,128)(2,1)} %x_ref.5, bf16[16,24,1664]{2,1,0:T(8,128)(2,1)} %pad_maximum_fusion.2.refs_0_, ...), custom_call_target="tpu_custom_call" | custom-call | flops 9000000 | bytes 1048576 | tf_op jit(solution)/shard_map/project_in/pallas_call | solution.py:440
  79.4 22.7 %attend_forward.1 = (bf16[1024,768]{1,0:T(8,128)(2,1)}, f32[16,1024]{1,0:T(8,128)}) custom-call(s32[1]{0:T(128)} %copy.129.length_ref, bf16[1024,2304]{1,0:T(8,128)(2,1)} %get-tuple-element.144.q_ref.k_ref.v_ref, bf16[1024,2304]{1,0:T(8,128)(2,1)} %get-tuple-element.144.q_ref.k_ref.v_ref, bf16[1024,2304]{1,0:T(8,128)(2,1)} %get-tuple-element.144.q_ref.k_ref.v_ref), custom_call_target="tpu_custom_call" | custom-call | flops 23000000 | bytes 1048576 | tf_op jit(solution)/shard_map/attend_forward/pallas_call | solution.py:281
  102.1 10.3 %collective-permute-done.9.in_far.out_far = bf16[2,768,768]{2,1,0:T(8,128)(2,1)} collective-permute-done((bf16[2,768,768]{2,1,0:T(8,128)(2,1)}, bf16[2,768,768]{2,1,0:T(8,128)(2,1)}, u32[]{:S(2)}, u32[]{:S(2)}) %collective-permute-start.9) | collective-permute-done | bytes 2359328 | tf_op jit(solution)/shard_map/ppermute | solution.py:47
  112.4 5.9 %project_out.1 = (f32[1024,768]{1,0:T(8,128)}, bf16[1024,768]{1,0:T(8,128)(2,1)}) custom-call(bf16[1024,768]{1,0:T(8,128)(2,1)} %x_ref.5, bf16[1024,768]{1,0:T(8,128)(2,1)} %get-tuple-element.147.o_ref.refs_2_, f32[8,768]{1,0:T(8,128)} %get-tuple-element.148.norm_ref, bf16[768,3328]{1,0:T(8,128)(2,1)} %get-tuple-element.149.weight_ref.router_ref), custom_call_target="tpu_custom_call" | custom-call | flops 7000000 | bytes 1048576 | tf_op jit(solution)/shard_map/project_out/pallas_call | solution.py:480
  118.3 3.8 convolution_convert_fusion
  123.4 4.4 all-to-all-start.1
  129.3 19.6 %all-to-all-done.1 = bf16[8,64,768]{2,1,0:T(8,128)(2,1)S(1)} async-done(((bf16[8,64,768]{2,1,0:T(8,128)(2,1)}), bf16[8,64,768]{2,1,0:T(8,128)(2,1)S(1)}, u32[]{:S(2)}, u32[]{:S(2)}) %all-to-all-start.1) | async-done | bytes 786464 | tf_op jit(solution)/shard_map/all_to_all | solution.py:59
  157.6 13.0 %expert_pass.4 = (bf16[2,512,768]{2,1,0:T(8,128)(2,1)}, bf16[2,512,768]{2,1,0:T(8,128)(2,1)}, bf16[512,768]{1,0:T(8,128)(2,1)}, f32[512,128]{1,0:T(8,128)}, bf16...) custom-call(s32[1]{0:T(128)} %bitcast.23.me_ref, bf16[512,768]{1,0:T(8,128)(2,1)} %bitcast.204, ...), custom_call_target="tpu_custom_call" | custom-call | flops 10000000 | bytes 1048576 | tf_op jit(solution)/shard_map/expert_pass/pallas_call | solution.py:740
  176.0 12.8 %expert_pass.5 = (bf16[2,512,768]{2,1,0:T(8,128)(2,1)}, bf16[2,512,768]{2,1,0:T(8,128)(2,1)}, bf16[512,768]{1,0:T(8,128)(2,1)}, f32[512,128]{1,0:T(8,128)}, bf16...) custom-call(s32[1]{0:T(128)} %bitcast.23.me_ref, bf16[512,768]{1,0:T(8,128)(2,1)} %bitcast.28.rows_ref, ...), custom_call_target="tpu_custom_call" | custom-call | flops 10000000 | bytes 1048576 | tf_op jit(solution)/shard_map/expert_pass/pallas_call | solution.py:740
  197.5 13.4 %expert_pass.6 = (bf16[2,512,768]{2,1,0:T(8,128)(2,1)}, bf16[2,512,768]{2,1,0:T(8,128)(2,1)}, bf16[512,768]{1,0:T(8,128)(2,1)}, f32[512,128]{1,0:T(8,128)}, bf16...) custom-call(s32[1]{0:T(128)} %bitcast.31.me_ref, bf16[512,768]{1,0:T(8,128)(2,1)} %bitcast.199, ...), custom_call_target="tpu_custom_call" | custom-call | flops 10000000 | bytes 1048576 | tf_op jit(solution)/shard_map/expert_pass/pallas_call | solution.py:740
  211.0 12.9 %expert_pass.7 = (bf16[2,512,768]{2,1,0:T(8,128)(2,1)}, bf16[2,512,768]{2,1,0:T(8,128)(2,1)}, bf16[512,768]{1,0:T(8,128)(2,1)}, f32[512,128]{1,0:T(8,128)}, bf16...) custom-call(s32[1]{0:T(128)} %bitcast.31.me_ref, bf16[512,768]{1,0:T(8,128)(2,1)} %bitcast.34.rows_ref, ...), custom_call_target="tpu_custom_call" | custom-call | flops 10000000 | bytes 1048576 | tf_op jit(solution)/shard_map/expert_pass/pallas_call | solution.py:740
  228.3 4.3 all-to-all-start.3
  248.7 4.9 %all-to-all-done.3 = bf16[8,64,768]{2,1,0:T(8,128)(2,1)S(1)} async-done(((bf16[8,64,768]{2,1,0:T(8,128)(2,1)}), bf16[8,64,768]{2,1,0:T(8,128)(2,1)S(1)}, u32[]{:S(2)}, u32[]{:S(2)}) %all-to-all-start.3) | async-done | bytes 786464 | tf_op jit(solution)/shard_map/all_to_all | solution.py:59
  267.1 11.1 %all-to-all-done.4 = bf16[8,64,768]{2,1,0:T(8,128)(2,1)S(1)} async-done(((bf16[8,64,768]{2,1,0:T(8,128)(2,1)}), bf16[8,64,768]{2,1,0:T(8,128)(2,1)S(1)}, u32[]{:S(2)}, u32[]{:S(2)}) %all-to-all-start.4) | async-done | bytes 786464 | tf_op jit(solution)/shard_map/all_to_all | solution.py:59
  279.1 12.1 %middle_back.1 = (f32[1024,768]{1,0:T(8,128)}, bf16[1024,768]{1,0:T(8,128)(2,1)}, bf16[1024,768]{1,0:T(8,128)(2,1)}, f32[16,1024]{1,0:T(8,128)}, f32[8,768]{1,0:T(8,128)}) custom-call(bf16[1024,1024]{1,0:T(8,128)(2,1)} %get-tuple-element.406.select_ref, bf16[512,768]{1,0:T(8,128)(2,1)} %bitcast.206, bf16[512,768]{1,0:T(8,128)(2,1)} %bitcast.207, ...), custom_call_target="tpu_custom_call" | custom-call | flops 12000000 | bytes 1048576 | tf_op jit(solution)/shard_map/middle_back/pallas_call | solution.py:526
  291.2 17.2 %attend_backward.3 = (bf16[1024,384]{1,0:T(8,128)(2,1)}, bf16[1024,384]{1,0:T(8,128)(2,1)}, bf16[1024,384]{1,0:T(8,128)(2,1)}) custom-call(s32[1]{0:T(128)} %copy.129.length_ref, bf16[1024,2304]{1,0:T(8,128)(2,1)} %get-tuple-element.144.q_ref.k_ref.v_ref, bf16[1024,2304]{1,0:T(8,128)(2,1)} %get-tuple-element.144.q_ref.k_ref.v_ref, ...), custom_call_target="tpu_custom_call" | custom-call | flops 17000000 | bytes 1048576 | tf_op jit(solution)/shard_map/attend_backward/pallas_call | solution.py:357
  308.5 9.6 %weight_sums.2 = (f32[384,2048]{1,0:T(8,128)}, bf16[384,2048]{1,0:T(8,128)(2,1)}) custom-call(s32[1]{0:T(128)} %bitcast.1.me_ref, bf16[1024,768]{1,0:T(8,128)(2,1)} %get-tuple-element.194.refs_0_, bf16[1024,768]{1,0:T(8,128)(2,1)} %get-tuple-element.195.refs_1_.refs_0_, bf16[1024,768]{1,0:T(8,128)(2,1)} %get-tuple-element.147.o_ref.refs_2_, ...), custom_call_target="tpu_custom_call" | custom-call | flops 6000000 | bytes 1048576 | tf_op jit(solution)/shard_map/weight_sums/pallas_call | solution.py:642
  334.4 12.3 %attend_backward.4 = (bf16[1024,256]{1,0:T(8,128)(2,1)}, bf16[1024,256]{1,0:T(8,128)(2,1)}, bf16[1024,256]{1,0:T(8,128)(2,1)}) custom-call(s32[1]{0:T(128)} %copy.129.length_ref, bf16[1024,2304]{1,0:T(8,128)(2,1)} %get-tuple-element.144.q_ref.k_ref.v_ref, bf16[1024,2304]{1,0:T(8,128)(2,1)} %get-tuple-element.144.q_ref.k_ref.v_ref, ...), custom_call_target="tpu_custom_call" | custom-call | flops 17000000 | bytes 1048576 | tf_op jit(solution)/shard_map/attend_backward/pallas_call | solution.py:357
  346.8 5.1 %fusion.111 = (bf16[384,2048]{1,0:T(8,128)(2,1)S(1)}, f32[384,2048]{1,0:T(8,128)}) fusion(f32[384,2048]{1,0:T(8,128)} %get-tuple-element.227, bf16[384,2048]{1,0:T(8,128)(2,1)} %collective-permute-done.18), kind=kLoop, calls=%fused_computation.195 | loop fusion | flops 2359296 | bytes 9437184 | tf_op jit(solution)/shard_map/convert.9
  357.9 7.0 %attend_backward.5 = (bf16[1024,128]{1,0:T(8,128)(2,1)}, bf16[1024,128]{1,0:T(8,128)(2,1)}, bf16[1024,128]{1,0:T(8,128)(2,1)}) custom-call(s32[1]{0:T(128)} %copy.129.length_ref, bf16[1024,2304]{1,0:T(8,128)(2,1)} %get-tuple-element.144.q_ref.k_ref.v_ref, bf16[1024,2304]{1,0:T(8,128)(2,1)} %get-tuple-element.144.q_ref.k_ref.v_ref, ...), custom_call_target="tpu_custom_call" | custom-call | flops 17000000 | bytes 1048576 | tf_op jit(solution)/shard_map/attend_backward/pallas_call | solution.py:357
  364.9 30.5 %collective-permute-done.20 = bf16[192,1024]{1,0:T(8,128)(2,1)} collective-permute-done((bf16[192,1024]{1,0:T(8,128)(2,1)}, bf16[192,1024]{1,0:T(8,128)(2,1)}, u32[]{:S(2)}, u32[]{:S(2)}) %collective-permute-start.20) | collective-permute-done | bytes 393248 | tf_op jit(solution)/shard_map/ppermute | solution.py:47
  403.8 4.9 %all-to-all-start.6 = ((bf16[8,64,768]{2,1,0:T(8,128)(2,1)}), bf16[8,64,768]{2,1,0:T(8,128)(2,1)}, u32[]{:S(2)}, u32[]{:S(2)}) async-start(bf16[8,64,768]{2,1,0:T(8,128)(2,1)} %bitcast.64), calls=%async_computation.6 | async-start | bytes 1572864 | tf_op jit(solution)/shard_map/all_to_all | solution.py:59
  408.8 11.4 %last_back.1 = (f32[1024,768]{1,0:T(8,128)}, f32[8,768]{1,0:T(8,128)}) custom-call(bf16[1024,768]{1,0:T(8,128)(2,1)} %x_ref.5, f32[1024,768]{1,0:T(8,128)} %get-tuple-element.223.grad_mid_ref, f32[8,768]{1,0:T(8,128)} %get-tuple-element.148.norm_ref, bf16[768,3328]{1,0:T(8,128)(2,1)} %get-tuple-element.149.weight_ref.router_ref, ...), custom_call_target="tpu_custom_call" | custom-call | flops 11000000 | bytes 1048576 | tf_op jit(solution)/shard_map/last_back/pallas_call | solution.py:573
  427.4 8.1 %multiply_add_fusion = (f32[1,768,768]{2,1,0:T(8,128)}, f32[1,768,768]{2,1,0:T(8,128)}, f32[1,768,768]{2,1,0:T(8,128)}, f32[1,768,768]{2,1,0:T(8,128)}) fusion(f32[1,768,768]{2,1,0:T(8,128)} %param.47, f32[1,768,768]{2,1,0:T(8,128)S(1)} %copy-done.5, f32[1,768,768]{2,1,0:T(8,128)} %param.46, bf16[2,768,768]{2,1,0:T(8,128)(2,1)} %collective-permute-done.34, ...), kind=kOutput, calls=%fused_computation.13 | convolution fusion | flops 611057664 | bytes 21626880 | tf_op jit(solution)/shard_map/dot_general | solution.py:30
  435.6 6.6 %weight_sums.3 = (f32[384,1280]{1,0:T(8,128)}, bf16[384,1280]{1,0:T(8,128)(2,1)}) custom-call(s32[1]{0:T(128)} %bitcast.1.me_ref, bf16[1024,768]{1,0:T(8,128)(2,1)} %get-tuple-element.195.refs_1_.refs_0_, bf16[1024,256]{1,0:T(8,128)(2,1)} %get-tuple-element.224.refs_3_.refs_1_, bf16[1024,128]{1,0:T(8,128)(2,1)} %get-tuple-element.233.refs_6_.refs_2_, ...), custom_call_target="tpu_custom_call" | custom-call | flops 6000000 | bytes 1048576 | tf_op jit(solution)/shard_map/weight_sums/pallas_call | solution.py:642
  442.2 9.0 %multiply_add_fusion.2 = (f32[1,768,768]{2,1,0:T(8,128)}, f32[1,768,768]{2,1,0:T(8,128)}, f32[1,768,768]{2,1,0:T(8,128)}, f32[1,768,768]{2,1,0:T(8,128)}) fusion(f32[1,768,768]{2,1,0:T(8,128)} %param.44, f32[1,768,768]{2,1,0:T(8,128)S(1)} %copy-done.7, f32[1,768,768]{2,1,0:T(8,128)} %param.43, bf16[2,768,768]{2,1,0:T(8,128)(2,1)} %collective-permute-done.34, ...), kind=kOutput, calls=%fused_computation.16 | convolution fusion | flops 611057664 | bytes 21626880 | tf_op jit(solution)/shard_map/dot_general | solution.py:30
  459.4 7.1 %collective-permute-done.29 = bf16[192,640]{1,0:T(8,128)(2,1)S(1)} collective-permute-done((bf16[192,640]{1,0:T(8,128)(2,1)S(1)}, bf16[192,640]{1,0:T(8,128)(2,1)S(1)}, u32[]{:S(2)}, u32[]{:S(2)}) %collective-permute-start.29) | collective-permute-done | bytes 245792 | tf_op jit(solution)/shard_map/ppermute | solution.py:47
  (316 shorter events, 163.6 us)
Async XLA Ops:
  4.9 13.7 %collective-permute-start.2 = (bf16[24,3328]{1,0:T(8,128)(2,1)}, bf16[24,3328]{1,0:T(8,128)(2,1)S(1)}, u32[]{:S(2)}, u32[]{:S(2)}) collective-permute-start(bf16[24,3328]{1,0:T(8,128)(2,1)} %concatenate.56), channel_id=1, source_target_pairs={{0,24},{4,28},{8,16},{12,20},{16,8},{20,12},{24,0},{28,4},{1,25},{... | collective-permute-start | bytes 479240 | tf_op jit(solution)/shard_map/ppermute | solution.py:47
  9.9 13.7 %collective-permute-start.1 = (bf16[24,3328]{1,0:T(8,128)(2,1)}, bf16[24,3328]{1,0:T(8,128)(2,1)S(1)}, u32[]{:S(2)}, u32[]{:S(2)}) collective-permute-start(bf16[24,3328]{1,0:T(8,128)(2,1)} %concatenate.56), channel_id=1, source_target_pairs={{0,16},{4,20},{8,24},{12,28},{16,0},{20,4},{24,8},{28,12},{1,17},{... | collective-permute-start | bytes 479240 | tf_op jit(solution)/shard_map/ppermute | solution.py:47
  9.9 13.7 %collective-permute-start = (bf16[24,3328]{1,0:T(8,128)(2,1)}, bf16[24,3328]{1,0:T(8,128)(2,1)S(1)}, u32[]{:S(2)}, u32[]{:S(2)}) collective-permute-start(bf16[24,3328]{1,0:T(8,128)(2,1)} %concatenate.56), channel_id=1, source_target_pairs={{0,8},{4,12},{8,0},{12,4},{16,24},{20,28},{24,16},{28,20},{1,9},{5... | collective-permute-start | bytes 479240 | tf_op jit(solution)/shard_map/ppermute | solution.py:47
  25.1 49.8 %all-to-all-start = ((bf16[2,8,64,896]{3,2,0,1:T(8,128)(2,1)}), bf16[2,8,64,896]{3,2,0,1:T(8,128)(2,1)}, u32[]{:S(2)}, u32[]{:S(2)}) async-start(bf16[2,8,64,896]{3,2,0,1:T(8,128)(2,1)} %copy.113), calls=%async_computation | async-start | bytes 3670016 | tf_op jit(solution)/shard_map/all_to_all | solution.py:59
  31.3 10.0 %collective-permute-start.3 = (bf16[4,24,1664]{2,1,0:T(8,128)(2,1)S(1)}, bf16[4,24,1664]{2,1,0:T(8,128)(2,1)S(1)}, u32[]{:S(2)}, u32[]{:S(2)}) collective-permute-start(bf16[4,24,1664]{2,1,0:T(8,128)(2,1)S(1)} %get-tuple-element.392), channel_id=1, source_target_pairs={{0,1},{1,0},{2,3},{3,2},{4,5},{5,4},{6,7},{7,6},{8,9},{9,8},{10,11... | collective-permute-start | bytes 958472 | tf_op jit(solution)/shard_map/ppermute | solution.py:47
  39.7 16.1 %collective-permute-start.6 = (bf16[8,24,1664]{2,1,0:T(8,128)(2,1)S(1)}, bf16[8,24,1664]{2,1,0:T(8,128)(2,1)S(1)}, u32[]{:S(2)}, u32[]{:S(2)}) collective-permute-start(bf16[8,24,1664]{2,1,0:T(8,128)(2,1)S(1)} %pad_maximum_fusion.7), channel_id=1, source_target_pairs={{0,1},{1,0},{2,3},{3,2},{4,5},{5,4},{6,7},{7,6},{8,9},{9,8},{10,11... | collective-permute-start | bytes 1916936 | tf_op jit(solution)/shard_map/ppermute | solution.py:47
  41.4 15.8 %collective-permute-start.4 = (bf16[8,24,1664]{2,1,0:T(8,128)(2,1)S(1)}, bf16[8,24,1664]{2,1,0:T(8,128)(2,1)S(1)}, u32[]{:S(2)}, u32[]{:S(2)}) collective-permute-start(bf16[8,24,1664]{2,1,0:T(8,128)(2,1)S(1)} %pad_maximum_fusion.6), channel_id=1, source_target_pairs={{0,2},{1,3},{2,0},{3,1},{4,6},{5,7},{6,4},{7,5},{8,10},{9,11},{10,... | collective-permute-start | bytes 1916936 | tf_op jit(solution)/shard_map/ppermute | solution.py:47
  58.9 53.5 %collective-permute-start.9 = (bf16[2,768,768]{2,1,0:T(8,128)(2,1)}, bf16[2,768,768]{2,1,0:T(8,128)(2,1)}, u32[]{:S(2)}, u32[]{:S(2)}) collective-permute-start(bf16[2,768,768]{2,1,0:T(8,128)(2,1)} %constant_dynamic-update-slice_fusion.in_own.out_own), channel_id=1, source_target_pairs={{0,1},{1,0},{2,3},{3,2},{4,5},{5,4},{6,7},{7,6},{8,9},{9,8},{10,11... | collective-permute-start | bytes 7077896 | tf_op jit(solution)/shard_map/ppermute | solution.py:47
  77.8 44.3 %collective-permute-start.10 = (bf16[1,1024,896]{2,1,0:T(8,128)(2,1)}, bf16[1,1024,896]{2,1,0:T(8,128)(2,1)}, u32[]{:S(2)}, u32[]{:S(2)}) collective-permute-start(bf16[1,1024,896]{2,1,0:T(8,128)(2,1)} %bitcast.18), channel_id=1, source_target_pairs={{0,2},{1,3},{2,0},{3,1},{4,6},{5,7},{6,4},{7,5},{8,10},{9,11},{10,... | collective-permute-start | bytes 5505032 | tf_op jit(solution)/shard_map/ppermute | solution.py:47
  123.4 25.4 %all-to-all-start.1 = ((bf16[8,64,768]{2,1,0:T(8,128)(2,1)}), bf16[8,64,768]{2,1,0:T(8,128)(2,1)S(1)}, u32[]{:S(2)}, u32[]{:S(2)}) async-start(bf16[8,64,768]{2,1,0:T(8,128)(2,1)} %bitcast.211), calls=%async_computation.1 | async-start | bytes 1572864 | tf_op jit(solution)/shard_map/all_to_all | solution.py:59
  127.9 69.6 %collective-permute-start.14 = (bf16[2,768,768]{2,1,0:T(8,128)(2,1)S(1)}, bf16[2,768,768]{2,1,0:T(8,128)(2,1)}, u32[]{:S(2)}, u32[]{:S(2)}) collective-permute-start(bf16[2,768,768]{2,1,0:T(8,128)(2,1)S(1)} %pad_maximum_fusion.in_own.out_own), channel_id=1, source_target_pairs={{0,1},{1,0},{2,3},{3,2},{4,5},{5,4},{6,7},{7,6},{8,9},{9,8},{10,11... | collective-permute-start | bytes 7077896 | tf_op jit(solution)/shard_map/ppermute | solution.py:47
  149.8 24.7 %all-to-all-start.2 = ((bf16[8,64,768]{2,1,0:T(8,128)(2,1)}), bf16[8,64,768]{2,1,0:T(8,128)(2,1)S(1)}, u32[]{:S(2)}, u32[]{:S(2)}) async-start(bf16[8,64,768]{2,1,0:T(8,128)(2,1)} %bitcast.209), calls=%async_computation.2 | async-start | bytes 1572864 | tf_op jit(solution)/shard_map/all_to_all | solution.py:59
  153.5 20.9 %collective-permute-start.11 = (bf16[1,512,768]{2,1,0:T(8,128)(2,1)}, bf16[1,512,768]{2,1,0:T(8,128)(2,1)}, u32[]{:S(2)}, u32[]{:S(2)}) collective-permute-start(bf16[1,512,768]{2,1,0:T(8,128)(2,1)} %bitcast.203), channel_id=1, source_target_pairs={{0,2},{1,3},{2,0},{3,1},{4,6},{5,7},{6,4},{7,5},{8,10},{9,11},{10,... | collective-permute-start | bytes 2359304 | tf_op jit(solution)/shard_map/ppermute | solution.py:47
  174.4 36.5 %collective-permute-start.13 = (bf16[1,512,768]{2,1,0:T(8,128)(2,1)S(1)}, bf16[1,512,768]{2,1,0:T(8,128)(2,1)}, u32[]{:S(2)}, u32[]{:S(2)}) collective-permute-start(bf16[1,512,768]{2,1,0:T(8,128)(2,1)S(1)} %bitcast.198), channel_id=1, source_target_pairs={{0,2},{1,3},{2,0},{3,1},{4,6},{5,7},{6,4},{7,5},{8,10},{9,11},{10,... | collective-permute-start | bytes 2359304 | tf_op jit(solution)/shard_map/ppermute | solution.py:47
  188.8 35.1 %collective-permute-start.12 = (bf16[1,512,768]{2,1,0:T(8,128)(2,1)}, bf16[1,512,768]{2,1,0:T(8,128)(2,1)}, u32[]{:S(2)}, u32[]{:S(2)}) collective-permute-start(bf16[1,512,768]{2,1,0:T(8,128)(2,1)} %bitcast.233), channel_id=1, source_target_pairs={{0,2},{1,3},{2,0},{3,1},{4,6},{5,7},{6,4},{7,5},{8,10},{9,11},{10,... | collective-permute-start | bytes 2359304 | tf_op jit(solution)/shard_map/ppermute | solution.py:47
  196.0 112.5 %collective-permute-start.16 = (bf16[1,512,768]{2,1,0:T(8,128)(2,1)}, bf16[1,512,768]{2,1,0:T(8,128)(2,1)}, u32[]{:S(2)}, u32[]{:S(2)}) collective-permute-start(bf16[1,512,768]{2,1,0:T(8,128)(2,1)} %fusion.22), channel_id=1, source_target_pairs={{0,2},{1,3},{2,0},{3,1},{4,6},{5,7},{6,4},{7,5},{8,10},{9,11},{10,... | collective-permute-start | bytes 2359304 | tf_op jit(solution)/shard_map/ppermute | solution.py:47
  223.9 22.6 %collective-permute-start.15 = (bf16[1,512,768]{2,1,0:T(8,128)(2,1)}, bf16[1,512,768]{2,1,0:T(8,128)(2,1)S(1)}, u32[]{:S(2)}, u32[]{:S(2)}) collective-permute-start(bf16[1,512,768]{2,1,0:T(8,128)(2,1)} %bitcast.234), channel_id=1, source_target_pairs={{0,2},{1,3},{2,0},{3,1},{4,6},{5,7},{6,4},{7,5},{8,10},{9,11},{10,... | collective-permute-start | bytes 2359304 | tf_op jit(solution)/shard_map/ppermute | solution.py:47
  228.3 25.3 %all-to-all-start.3 = ((bf16[8,64,768]{2,1,0:T(8,128)(2,1)}), bf16[8,64,768]{2,1,0:T(8,128)(2,1)S(1)}, u32[]{:S(2)}, u32[]{:S(2)}) async-start(bf16[8,64,768]{2,1,0:T(8,128)(2,1)} %bitcast.36), calls=%async_computation.3 | async-start | bytes 1572864 | tf_op jit(solution)/shard_map/all_to_all | solution.py:59
  237.8 70.6 %collective-permute-start.17 = (bf16[1,512,768]{2,1,0:T(8,128)(2,1)}, bf16[1,512,768]{2,1,0:T(8,128)(2,1)}, u32[]{:S(2)}, u32[]{:S(2)}) collective-permute-start(bf16[1,512,768]{2,1,0:T(8,128)(2,1)} %fusion.40), channel_id=1, source_target_pairs={{0,2},{1,3},{2,0},{3,1},{4,6},{5,7},{6,4},{7,5},{8,10},{9,11},{10,... | collective-permute-start | bytes 2359304 | tf_op jit(solution)/shard_map/ppermute | solution.py:47
  253.6 24.6 %all-to-all-start.4 = ((bf16[8,64,768]{2,1,0:T(8,128)(2,1)}), bf16[8,64,768]{2,1,0:T(8,128)(2,1)S(1)}, u32[]{:S(2)}, u32[]{:S(2)}) async-start(bf16[8,64,768]{2,1,0:T(8,128)(2,1)} %bitcast.210), calls=%async_computation.4 | async-start | bytes 1572864 | tf_op jit(solution)/shard_map/all_to_all | solution.py:59
  318.0 28.7 %collective-permute-start.18 = (bf16[384,2048]{1,0:T(8,128)(2,1)}, bf16[384,2048]{1,0:T(8,128)(2,1)}, u32[]{:S(2)}, u32[]{:S(2)}) collective-permute-start(bf16[384,2048]{1,0:T(8,128)(2,1)} %get-tuple-element.211), channel_id=1, source_target_pairs={{0,4},{4,0},{8,12},{12,8},{16,20},{20,16},{24,28},{28,24},{1,5},{5... | collective-permute-start | bytes 4718600 | tf_op jit(solution)/shard_map/ppermute | solution.py:47
  320.9 25.8 %all-to-all-start.5 = ((bf16[8,64,768]{2,1,0:T(8,128)(2,1)}), bf16[8,64,768]{2,1,0:T(8,128)(2,1)S(1)}, u32[]{:S(2)}, u32[]{:S(2)}) async-start(bf16[8,64,768]{2,1,0:T(8,128)(2,1)} %bitcast.59), calls=%async_computation.5 | async-start | bytes 1572864 | tf_op jit(solution)/shard_map/all_to_all | solution.py:59
  333.0 94.4 %collective-permute-start.34 = (bf16[2,768,768]{2,1,0:T(8,128)(2,1)}, bf16[2,768,768]{2,1,0:T(8,128)(2,1)}, u32[]{:S(2)}, u32[]{:S(2)}) collective-permute-start(bf16[2,768,768]{2,1,0:T(8,128)(2,1)} %pad_maximum_fusion.1), channel_id=1, source_target_pairs={{0,1},{1,0},{2,3},{3,2},{4,5},{5,4},{6,7},{7,6},{8,9},{9,8},{10,11... | collective-permute-start | bytes 7077896 | tf_op jit(solution)/shard_map/ppermute | solution.py:47
  352.7 42.7 %collective-permute-start.20 = (bf16[192,1024]{1,0:T(8,128)(2,1)}, bf16[192,1024]{1,0:T(8,128)(2,1)}, u32[]{:S(2)}, u32[]{:S(2)}) collective-permute-start(bf16[192,1024]{1,0:T(8,128)(2,1)} %get-tuple-element.385), channel_id=1, source_target_pairs={{0,1},{1,0},{2,3},{3,2},{4,5},{5,4},{6,7},{7,6},{8,9},{9,8},{10,11... | collective-permute-start | bytes 1179656 | tf_op jit(solution)/shard_map/ppermute | solution.py:47
  353.4 42.0 %collective-permute-start.19 = (bf16[192,1024]{1,0:T(8,128)(2,1)S(1)}, bf16[192,1024]{1,0:T(8,128)(2,1)}, u32[]{:S(2)}, u32[]{:S(2)}) collective-permute-start(bf16[192,1024]{1,0:T(8,128)(2,1)S(1)} %get-tuple-element.386), channel_id=1, source_target_pairs={{0,2},{1,3},{2,0},{3,1},{4,6},{5,7},{6,4},{7,5},{8,10},{9,11},{10,... | collective-permute-start | bytes 1179656 | tf_op jit(solution)/shard_map/ppermute | solution.py:47
  398.5 21.6 %collective-permute-start.22 = (bf16[96,1024]{1,0:T(8,128)(2,1)S(1)}, bf16[96,1024]{1,0:T(8,128)(2,1)S(1)}, u32[]{:S(2)}, u32[]{:S(2)}) collective-permute-start(bf16[96,1024]{1,0:T(8,128)(2,1)S(1)} %slice.440), channel_id=1, source_target_pairs={{0,2},{1,3},{2,0},{3,1},{4,6},{5,7},{6,4},{7,5},{8,10},{9,11},{10,... | collective-permute-start | bytes 589832 | tf_op jit(solution)/shard_map/ppermute | solution.py:47
  400.1 20.0 %collective-permute-start.21 = (bf16[96,1024]{1,0:T(8,128)(2,1)S(1)}, bf16[96,1024]{1,0:T(8,128)(2,1)S(1)}, u32[]{:S(2)}, u32[]{:S(2)}) collective-permute-start(bf16[96,1024]{1,0:T(8,128)(2,1)S(1)} %slice.441), channel_id=1, source_target_pairs={{0,1},{1,0},{2,3},{3,2},{4,5},{5,4},{6,7},{7,6},{8,9},{9,8},{10,11... | collective-permute-start | bytes 589832 | tf_op jit(solution)/shard_map/ppermute | solution.py:47
  403.8 47.4 %all-to-all-start.6 = ((bf16[8,64,768]{2,1,0:T(8,128)(2,1)}), bf16[8,64,768]{2,1,0:T(8,128)(2,1)}, u32[]{:S(2)}, u32[]{:S(2)}) async-start(bf16[8,64,768]{2,1,0:T(8,128)(2,1)} %bitcast.64), calls=%async_computation.6 | async-start | bytes 1572864 | tf_op jit(solution)/shard_map/all_to_all | solution.py:59
  423.0 19.1 %collective-permute-start.25 = (bf16[24,2048]{1,0:T(8,128)(2,1)}, bf16[24,2048]{1,0:T(8,128)(2,1)S(1)}, u32[]{:S(2)}, u32[]{:S(2)}) collective-permute-start(bf16[24,2048]{1,0:T(8,128)(2,1)} %get-tuple-element.393), channel_id=1, source_target_pairs={{0,24},{4,28},{8,16},{12,20},{16,8},{20,12},{24,0},{28,4},{1,25},{... | collective-permute-start | bytes 294920 | tf_op jit(solution)/shard_map/ppermute | solution.py:47
  426.9 15.3 %collective-permute-start.24 = (bf16[24,2048]{1,0:T(8,128)(2,1)}, bf16[24,2048]{1,0:T(8,128)(2,1)S(1)}, u32[]{:S(2)}, u32[]{:S(2)}) collective-permute-start(bf16[24,2048]{1,0:T(8,128)(2,1)} %get-tuple-element.394), channel_id=1, source_target_pairs={{0,16},{4,20},{8,24},{12,28},{16,0},{20,4},{24,8},{28,12},{1,17},{... | collective-permute-start | bytes 294920 | tf_op jit(solution)/shard_map/ppermute | solution.py:47
  426.9 15.3 %collective-permute-start.23 = (bf16[24,2048]{1,0:T(8,128)(2,1)S(1)}, bf16[24,2048]{1,0:T(8,128)(2,1)S(1)}, u32[]{:S(2)}, u32[]{:S(2)}) collective-permute-start(bf16[24,2048]{1,0:T(8,128)(2,1)S(1)} %get-tuple-element.395), channel_id=1, source_target_pairs={{0,8},{4,12},{8,0},{12,4},{16,24},{20,28},{24,16},{28,20},{1,9},{5... | collective-permute-start | bytes 294920 | tf_op jit(solution)/shard_map/ppermute | solution.py:47
  442.1 14.3 %collective-permute-start.26 = (bf16[384,1280]{1,0:T(8,128)(2,1)}, bf16[384,1280]{1,0:T(8,128)(2,1)}, u32[]{:S(2)}, u32[]{:S(2)}) collective-permute-start(bf16[384,1280]{1,0:T(8,128)(2,1)} %get-tuple-element.247), channel_id=1, source_target_pairs={{0,4},{4,0},{8,12},{12,8},{16,20},{20,16},{24,28},{28,24},{1,5},{5... | collective-permute-start | bytes 2949128 | tf_op jit(solution)/shard_map/ppermute | solution.py:47
  (79 other events, 461.0 us)
